TPU v7x, 32 devices: a whole 2x2x4 slice. The times are simulated.
32 devices in a mesh: seq: 2 (over core), shard: 16 (over z, y, x).
Axes of the slice: x: 2, y: 2, z: 4, core: 2. Of those that a mesh axis runs over, the one named last changes fastest.
Arguments:
- tokens: bfloat16 [16, 2048, 768], P('shard', 'seq'), may hold values from -6 to 6
- lengths: int32 [16, 8], P('shard'), may hold values from 1 to 1024, 2048 in all within a row
- query_weight: bfloat16 [768, 768], P(('seq', 'shard')), may hold values from -0.21875 to 0.21875
- query_bias: bfloat16 [768], P(('seq', 'shard')), may hold values from -3 to 3
- key_weight: bfloat16 [768, 768], P(('seq', 'shard')), may hold values from -0.21875 to 0.21875
- value_weight: bfloat16 [768, 768], P(('seq', 'shard')), may hold values from -0.21875 to 0.21875
- value_bias: bfloat16 [768], P(('seq', 'shard')), may hold values from -3 to 3
- output_weight: bfloat16 [768, 768], P(('seq', 'shard')), may hold values from -1.25 to 1.25
- output_bias: bfloat16 [768], P(('seq', 'shard')), may hold values from -3 to 3
- first_gain: bfloat16 [768], P(('seq', 'shard')), may hold values from 0.5 to 1.5
- first_shift: bfloat16 [768], P(('seq', 'shard')), may hold values from -3 to 3
- up_weight: bfloat16 [768, 3072], P(('seq', 'shard')), may hold values from -0.21875 to 0.21875
- up_bias: bfloat16 [3072], P(('seq', 'shard')), may hold values from -3 to 3
- down_weight: bfloat16 [3072, 768], P(('seq', 'shard')), may hold values from -0.109375 to 0.109375
- down_bias: bfloat16 [768], P(('seq', 'shard')), may hold values from -3 to 3
- second_gain: bfloat16 [768], P(('seq', 'shard')), may hold values from 0.5 to 1.5
- second_shift: bfloat16 [768], P(('seq', 'shard')), may hold values from -3 to 3
- cotangent: bfloat16 [16, 2048, 768], P('shard', 'seq'), may hold values from -6 to 6
Outputs:
- output: bfloat16 [16, 2048, 768], P('shard', 'seq')
- grad_tokens: float32 [16, 2048, 768], P('shard', 'seq')
- grad_query_weight: float32 [768, 768], P(('seq', 'shard'))
- grad_query_bias: float32 [768], P(('seq', 'shard'))
- grad_key_weight: float32 [768, 768], P(('seq', 'shard'))
- grad_value_weight: float32 [768, 768], P(('seq', 'shard'))
- grad_value_bias: float32 [768], P(('seq', 'shard'))
- grad_output_weight: float32 [768, 768], P(('seq', 'shard'))
- grad_output_bias: float32 [768], P(('seq', 'shard'))
- grad_first_gain: float32 [768], P(('seq', 'shard'))
- grad_first_shift: float32 [768], P(('seq', 'shard'))
- grad_up_weight: float32 [768, 3072], P(('seq', 'shard'))
- grad_up_bias: float32 [3072], P(('seq', 'shard'))
- grad_down_weight: float32 [3072, 768], P(('seq', 'shard'))
- grad_down_bias: float32 [768], P(('seq', 'shard'))
- grad_second_gain: float32 [768], P(('seq', 'shard'))
- grad_second_shift: float32 [768], P(('seq', 'shard'))
Inputs may be any that keep to these rules, and one draw needn't show every extreme that they name: Each sequence's 8 document lengths add up to 2048, and one of them is exactly 1024.
All inputs are finite; a program needn't handle non-finite values.
Results may differ from a plain program's by a relative error of at most 0.014.
Values may be sent and summed in bfloat16 or wider, within the bound.
No kernel may reach another device: no remote copies, remote signals or barrier semaphores. Data moves between devices by JAX's collectives and lax.ppermute only.
A program may use at most 192 MiB of HBM per device.

v0:
```python
from functools import partial

import jax
import jax.numpy as jnp
from jax import lax
from jax.sharding import PartitionSpec as P

HEADS = 12
HEAD_DIM = 64


def matmul(left, right):
    return jnp.dot(left, right, preferred_element_type=jnp.float32)


def matmul_left(left, right):
    return lax.dot_general(
        left, right, (((0,), (0,)), ((), ())), preferred_element_type=jnp.float32
    )


def matmul_right(left, right):
    return lax.dot_general(
        left, right, (((1,), (1,)), ((), ())), preferred_element_type=jnp.float32
    )


def layer_norm(hidden, gain, shift):
    centred = hidden - jnp.mean(hidden, axis=-1, keepdims=True)
    factor = lax.rsqrt(jnp.mean(centred * centred, axis=-1, keepdims=True) + 1e-12)
    normed = centred * factor
    return (normed * gain + shift, normed, factor)


def norm_back(grad, normed, factor, gain):
    scaled = grad * gain
    inner = (
        scaled
        - jnp.mean(scaled, axis=-1, keepdims=True)
        - normed * jnp.mean(scaled * normed, axis=-1, keepdims=True)
    )
    return (factor * inner, jnp.sum(grad * normed, axis=0), jnp.sum(grad, axis=0))


def doc_index(lengths, count):
    ends = jnp.cumsum(lengths, axis=-1)
    places = jnp.arange(count, dtype=jnp.int32)
    return jnp.sum((places[None, :, None] >= ends[:, None, :]).astype(jnp.int32), axis=-1)


def split_heads(block, heads):
    return block.reshape(block.shape[0], block.shape[1], heads, block.shape[2] // heads)


def take_rows(array, index, size):
    return lax.dynamic_slice_in_dim(array, index * size, size, 1)


def masked_scores(query_blk, key_blk, query_doc, key_doc, scale):
    scores = (
        jnp.einsum("sqhd,skhd->shqk", query_blk, key_blk, preferred_element_type=jnp.float32)
        * scale
    )
    same = query_doc[:, None, :, None] == key_doc[:, None, None, :]
    return (jnp.where(same, scores, -1e30), same)


def attend(query, keys, values, doc, heads, scale):
    seq_count, count, width = query.shape
    size = min(512, count)
    blocks = count // size
    order = jnp.arange(blocks, dtype=jnp.int32)

    def one_query(index):
        query_blk = split_heads(take_rows(query, index, size), heads)
        query_doc = take_rows(doc, index, size)

        def peak_step(carry, key_index):
            running_top, total = carry
            scores, same = masked_scores(
                query_blk,
                split_heads(take_rows(keys, key_index, size), heads),
                query_doc,
                take_rows(doc, key_index, size),
                scale,
            )
            new_top = jnp.maximum(running_top, jnp.max(scores, axis=-1))
            weights_now = jnp.where(same, jnp.exp(scores - new_top[..., None]), 0.0)
            return (
                (new_top, total * jnp.exp(running_top - new_top) + jnp.sum(weights_now, axis=-1)),
                None,
            )

        start_carry = (
            jnp.full((seq_count, heads, size), -1e30, jnp.float32),
            jnp.zeros((seq_count, heads, size), jnp.float32),
        )
        (running_top, total), _ = lax.scan(peak_step, start_carry, order)
        log_sum = running_top + jnp.log(total)

        def value_step(summed, key_index):
            scores, _ = masked_scores(
                query_blk,
                split_heads(take_rows(keys, key_index, size), heads),
                query_doc,
                take_rows(doc, key_index, size),
                scale,
            )
            attn_prob = jnp.exp(scores - log_sum[..., None]).astype(jnp.bfloat16)
            value_blk = split_heads(take_rows(values, key_index, size), heads)
            return (
                summed
                + jnp.einsum(
                    "shqk,skhd->sqhd", attn_prob, value_blk, preferred_element_type=jnp.float32
                ),
                None,
            )

        summed, _ = lax.scan(
            value_step, jnp.zeros((seq_count, size, heads, width // heads), jnp.float32), order
        )
        return (summed.reshape(seq_count, size, width), log_sum)

    pieces, log_sums = lax.map(one_query, order)
    return (jnp.moveaxis(pieces, 0, 1).reshape(seq_count, count, width), log_sums)


def attend_back(query, keys, values, doc, log_sums, grad_heads, delta, heads, scale):
    seq_count, count, width = query.shape
    size = min(512, count)
    blocks = count // size
    head_width = width // heads
    order = jnp.arange(blocks, dtype=jnp.int32)

    def one_key(grad_query, key_index):
        key_blk = split_heads(take_rows(keys, key_index, size), heads)
        value_blk = split_heads(take_rows(values, key_index, size), heads)
        key_doc = take_rows(doc, key_index, size)

        def query_step(carry, index):
            grad_key, grad_value, grad_rows = carry
            query_blk = split_heads(take_rows(query, index, size), heads)
            grad_blk = split_heads(take_rows(grad_heads, index, size), heads)
            scores, _ = masked_scores(
                query_blk, key_blk, take_rows(doc, index, size), key_doc, scale
            )
            log_sum = lax.dynamic_index_in_dim(log_sums, index, 0, keepdims=False)
            attn_prob = jnp.exp(scores - log_sum[..., None])
            grad_value = grad_value + jnp.einsum(
                "shqk,sqhd->skhd",
                attn_prob.astype(jnp.bfloat16),
                grad_blk,
                preferred_element_type=jnp.float32,
            )
            grad_prob = jnp.einsum(
                "sqhd,skhd->shqk", grad_blk, value_blk, preferred_element_type=jnp.float32
            )
            delta_blk = jnp.swapaxes(take_rows(delta, index, size), 1, 2)
            grad_scores = (attn_prob * (grad_prob - delta_blk[..., None])).astype(jnp.bfloat16)
            grad_key = (
                grad_key
                + jnp.einsum(
                    "shqk,sqhd->skhd", grad_scores, query_blk, preferred_element_type=jnp.float32
                )
                * scale
            )
            part = (
                jnp.einsum(
                    "shqk,skhd->sqhd", grad_scores, key_blk, preferred_element_type=jnp.float32
                )
                * scale
            )
            grad_rows = lax.dynamic_update_slice_in_dim(
                grad_rows, take_rows(grad_rows, index, size) + part, index * size, 1
            )
            return ((grad_key, grad_value, grad_rows), None)

        zeros_blk = jnp.zeros((seq_count, size, heads, head_width), jnp.float32)
        (grad_key, grad_value, grad_query), _ = lax.scan(
            query_step, (zeros_blk, zeros_blk, grad_query), order
        )
        return (
            grad_query,
            (grad_key.reshape(seq_count, size, width), grad_value.reshape(seq_count, size, width)),
        )

    grad_query, (key_parts, value_parts) = lax.scan(
        one_key, jnp.zeros((seq_count, count, heads, head_width), jnp.float32), order
    )
    grad_keys = jnp.moveaxis(key_parts, 0, 1).reshape(seq_count, count, width)
    grad_values = jnp.moveaxis(value_parts, 0, 1).reshape(seq_count, count, width)
    return (grad_query.reshape(seq_count, count, width), grad_keys, grad_values)


def on_device(
    tokens,
    lengths,
    query_weight,
    query_bias,
    key_weight,
    value_weight,
    value_bias,
    output_weight,
    output_bias,
    first_gain,
    first_shift,
    up_weight,
    up_bias,
    down_weight,
    down_bias,
    second_gain,
    second_shift,
    cotangent,
):
    seq_count, half_len, width = tokens.shape
    row_count = seq_count * half_len
    heads_here = HEADS // lax.axis_size("seq")
    scale = HEAD_DIM ** (-0.5)
    (
        w_query,
        w_key,
        w_value,
        w_out,
        w_up,
        w_down,
        b_query,
        b_value,
        b_out,
        gain_one,
        shift_one,
        b_up,
        b_down,
        gain_two,
        shift_two,
    ) = (
        lax.all_gather(query_weight, ("seq", "shard"), axis=0, tiled=True),
        lax.all_gather(key_weight, ("seq", "shard"), axis=0, tiled=True),
        lax.all_gather(value_weight, ("seq", "shard"), axis=0, tiled=True),
        lax.all_gather(output_weight, ("seq", "shard"), axis=0, tiled=True),
        lax.all_gather(up_weight, ("seq", "shard"), axis=0, tiled=True),
        lax.all_gather(down_weight, ("seq", "shard"), axis=0, tiled=True),
        lax.all_gather(query_bias, ("seq", "shard"), axis=0, tiled=True),
        lax.all_gather(value_bias, ("seq", "shard"), axis=0, tiled=True),
        lax.all_gather(output_bias, ("seq", "shard"), axis=0, tiled=True),
        lax.all_gather(first_gain, ("seq", "shard"), axis=0, tiled=True),
        lax.all_gather(first_shift, ("seq", "shard"), axis=0, tiled=True),
        lax.all_gather(up_bias, ("seq", "shard"), axis=0, tiled=True),
        lax.all_gather(down_bias, ("seq", "shard"), axis=0, tiled=True),
        lax.all_gather(second_gain, ("seq", "shard"), axis=0, tiled=True),
        lax.all_gather(second_shift, ("seq", "shard"), axis=0, tiled=True),
    )
    gain_one = gain_one.astype(jnp.float32)
    gain_two = gain_two.astype(jnp.float32)
    flat = tokens.reshape(row_count, width)
    query = (matmul(flat, w_query) + b_query.astype(jnp.float32)).astype(jnp.bfloat16)
    keys = matmul(flat, w_key).astype(jnp.bfloat16)
    values = (matmul(flat, w_value) + b_value.astype(jnp.float32)).astype(jnp.bfloat16)
    query_h, keys_h, values_h = (
        lax.all_to_all(
            query.reshape(seq_count, half_len, width),
            "seq",
            split_axis=2,
            concat_axis=1,
            tiled=True,
        ),
        lax.all_to_all(
            keys.reshape(seq_count, half_len, width), "seq", split_axis=2, concat_axis=1, tiled=True
        ),
        lax.all_to_all(
            values.reshape(seq_count, half_len, width),
            "seq",
            split_axis=2,
            concat_axis=1,
            tiled=True,
        ),
    )
    doc = doc_index(lengths, half_len * lax.axis_size("seq"))
    attn_f32, log_sums = attend(query_h, keys_h, values_h, doc, heads_here, scale)
    mixed = lax.all_to_all(
        attn_f32.astype(jnp.bfloat16), "seq", split_axis=1, concat_axis=2, tiled=True
    ).reshape(row_count, width)
    branch = matmul(mixed, w_out) + b_out.astype(jnp.float32)
    first, normed_one, factor_one = layer_norm(
        flat.astype(jnp.float32) + branch, gain_one, shift_one.astype(jnp.float32)
    )
    first_low = first.astype(jnp.bfloat16)
    preact = matmul(first_low, w_up) + b_up.astype(jnp.float32)
    activated, gelu_back = jax.vjp(partial(jax.nn.gelu, approximate=False), preact)
    act_low = activated.astype(jnp.bfloat16)
    second_in = first + matmul(act_low, w_down) + b_down.astype(jnp.float32)
    result, normed_two, factor_two = layer_norm(second_in, gain_two, shift_two.astype(jnp.float32))
    output = result.astype(jnp.bfloat16).reshape(seq_count, half_len, width)
    w_query, w_key, w_value, w_out, w_up, w_down, gain_one, gain_two = (
        lax.all_gather(query_weight, ("seq", "shard"), axis=0, tiled=True),
        lax.all_gather(key_weight, ("seq", "shard"), axis=0, tiled=True),
        lax.all_gather(value_weight, ("seq", "shard"), axis=0, tiled=True),
        lax.all_gather(output_weight, ("seq", "shard"), axis=0, tiled=True),
        lax.all_gather(up_weight, ("seq", "shard"), axis=0, tiled=True),
        lax.all_gather(down_weight, ("seq", "shard"), axis=0, tiled=True),
        lax.all_gather(first_gain, ("seq", "shard"), axis=0, tiled=True),
        lax.all_gather(second_gain, ("seq", "shard"), axis=0, tiled=True),
    )
    gain_one = gain_one.astype(jnp.float32)
    gain_two = gain_two.astype(jnp.float32)
    grad_y = cotangent.reshape(row_count, width).astype(jnp.float32)
    g_second, d_gain_two, d_shift_two = norm_back(grad_y, normed_two, factor_two, gain_two)
    g_down = g_second.astype(jnp.bfloat16)
    d_w_down = matmul_left(act_low, g_down)
    d_b_down = jnp.sum(g_down.astype(jnp.float32), axis=0)
    g_pre = gelu_back(matmul_right(g_down, w_down))[0].astype(jnp.bfloat16)
    d_w_up = matmul_left(first_low, g_pre)
    d_b_up = jnp.sum(g_pre.astype(jnp.float32), axis=0)
    g_first = g_second + matmul_right(g_pre, w_up)
    g_res, d_gain_one, d_shift_one = norm_back(g_first, normed_one, factor_one, gain_one)
    g_branch = g_res.astype(jnp.bfloat16)
    d_w_out = matmul_left(mixed, g_branch)
    d_b_out = jnp.sum(g_branch.astype(jnp.float32), axis=0)
    g_mixed = matmul_right(g_branch, w_out).astype(jnp.bfloat16)
    grad_heads = lax.all_to_all(
        g_mixed.reshape(seq_count, half_len, width), "seq", split_axis=2, concat_axis=1, tiled=True
    )
    count = grad_heads.shape[1]
    delta = jnp.sum(
        (grad_heads.astype(jnp.float32) * attn_f32).reshape(seq_count, count, heads_here, -1),
        axis=-1,
    )
    g_query, g_keys, g_values = attend_back(
        query_h, keys_h, values_h, doc, log_sums, grad_heads, delta, heads_here, scale
    )
    back_query, back_keys, back_values = (
        lax.all_to_all(
            g_query.astype(jnp.bfloat16), "seq", split_axis=1, concat_axis=2, tiled=True
        ),
        lax.all_to_all(g_keys.astype(jnp.bfloat16), "seq", split_axis=1, concat_axis=2, tiled=True),
        lax.all_to_all(
            g_values.astype(jnp.bfloat16), "seq", split_axis=1, concat_axis=2, tiled=True
        ),
    )
    back_query = back_query.reshape(row_count, width)
    back_keys = back_keys.reshape(row_count, width)
    back_values = back_values.reshape(row_count, width)
    d_w_query = matmul_left(flat, back_query)
    d_b_query = jnp.sum(back_query.astype(jnp.float32), axis=0)
    d_w_key = matmul_left(flat, back_keys)
    d_w_value = matmul_left(flat, back_values)
    d_b_value = jnp.sum(back_values.astype(jnp.float32), axis=0)
    grad_tokens = (
        g_res
        + matmul_right(back_query, w_query)
        + matmul_right(back_keys, w_key)
        + matmul_right(back_values, w_value)
    )
    grad_tokens = grad_tokens.reshape(seq_count, half_len, width)
    (
        r_w_query,
        r_b_query,
        r_w_key,
        r_w_value,
        r_b_value,
        r_w_out,
        r_b_out,
        r_gain_one,
        r_shift_one,
        r_w_up,
        r_b_up,
        r_w_down,
        r_b_down,
        r_gain_two,
        r_shift_two,
    ) = (
        lax.psum_scatter(d_w_query, ("seq", "shard"), scatter_dimension=0, tiled=True),
        lax.psum_scatter(d_b_query, ("seq", "shard"), scatter_dimension=0, tiled=True),
        lax.psum_scatter(d_w_key, ("seq", "shard"), scatter_dimension=0, tiled=True),
        lax.psum_scatter(d_w_value, ("seq", "shard"), scatter_dimension=0, tiled=True),
        lax.psum_scatter(d_b_value, ("seq", "shard"), scatter_dimension=0, tiled=True),
        lax.psum_scatter(d_w_out, ("seq", "shard"), scatter_dimension=0, tiled=True),
        lax.psum_scatter(d_b_out, ("seq", "shard"), scatter_dimension=0, tiled=True),
        lax.psum_scatter(d_gain_one, ("seq", "shard"), scatter_dimension=0, tiled=True),
        lax.psum_scatter(d_shift_one, ("seq", "shard"), scatter_dimension=0, tiled=True),
        lax.psum_scatter(d_w_up, ("seq", "shard"), scatter_dimension=0, tiled=True),
        lax.psum_scatter(d_b_up, ("seq", "shard"), scatter_dimension=0, tiled=True),
        lax.psum_scatter(d_w_down, ("seq", "shard"), scatter_dimension=0, tiled=True),
        lax.psum_scatter(d_b_down, ("seq", "shard"), scatter_dimension=0, tiled=True),
        lax.psum_scatter(d_gain_two, ("seq", "shard"), scatter_dimension=0, tiled=True),
        lax.psum_scatter(d_shift_two, ("seq", "shard"), scatter_dimension=0, tiled=True),
    )
    return (
        output,
        grad_tokens,
        r_w_query,
        r_b_query,
        r_w_key,
        r_w_value,
        r_b_value,
        r_w_out,
        r_b_out,
        r_gain_one,
        r_shift_one,
        r_w_up,
        r_b_up,
        r_w_down,
        r_b_down,
        r_gain_two,
        r_shift_two,
    )


def solution(mesh):
    return jax.shard_map(
        on_device,
        mesh=mesh,
        in_specs=(
            P("shard", "seq", None),
            P("shard", None),
            P(("seq", "shard"), None),
            P(("seq", "shard")),
            P(("seq", "shard"), None),
            P(("seq", "shard"), None),
            P(("seq", "shard")),
            P(("seq", "shard"), None),
            P(("seq", "shard")),
            P(("seq", "shard")),
            P(("seq", "shard")),
            P(("seq", "shard"), None),
            P(("seq", "shard")),
            P(("seq", "shard"), None),
            P(("seq", "shard")),
            P(("seq", "shard")),
            P(("seq", "shard")),
            P("shard", "seq", None),
        ),
        out_specs=(
            P("shard", "seq", None),
            P("shard", "seq", None),
            P(("seq", "shard"), None),
            P(("seq", "shard")),
            P(("seq", "shard"), None),
            P(("seq", "shard"), None),
            P(("seq", "shard")),
            P(("seq", "shard"), None),
            P(("seq", "shard")),
            P(("seq", "shard")),
            P(("seq", "shard")),
            P(("seq", "shard"), None),
            P(("seq", "shard")),
            P(("seq", "shard"), None),
            P(("seq", "shard")),
            P(("seq", "shard")),
            P(("seq", "shard")),
        ),
        check_vma=False,
    )
```

profile of v0, /device:TPU:0, one launch (start us, length us, event | category | flops | bytes accessed | tf_op | source)
XLA Modules:
  0.0 1882.8 jit_solution(12113288116937162095)
XLA Ops:
  18.8 42.4 %all-reduce.19 = (bf16[768]{0:T(1024)(128)(2,1)S(1)}, bf16[768]{0:T(1024)(128)(2,1)S(1)}, bf16[768]{0:T(1024)(128)(2,1)S(1)}, bf16[768]{0:T(1024)(128)(2,1)S(1)}...) all-reduce(bf16[768]{0:T(1024)(128)(2,1)S(1)} %dynamic-update-slice, ...), channel_id=1, replica_groups=mesh['seq'=2,'shard'=16] {'seq','shard'}, use_global_device_ids=true, to_apply=%add | all-reduce | flops 9216 | bytes 36864
  109.7 14.3 all-gather.11.cloned.1.call-done
  162.2 17.8 all-gather.9.cloned.1.call-done
  218.7 281.3 %while.72 = (s32[]{:T(128)}, f32[4,1,512,384]{2,3,1,0:T(8,128)}, f32[4,1,6,512]{3,2,1,0:T(8,128)}, s32[4]{0:T(128)S(1)}, bf16[1,2048,384]{1,2,0:T(8,128)(2,1)}, ...) while((s32[]{:T(128)}, f32[4,1,512,384]{2,3,1,0:T(8,128)}, ...), condition=%wide.region_9.10_spmd.clone, body=%wide.region_2.9_spmd.clone.sunk | while | flops 623790080 | bytes 22398808 | solution.py:124
  221.1 38.9 %while.75 = (s32[]{:T(128)}, f32[1,6,512]{2,1,0:T(8,128)S(1)}, f32[1,6,512]{2,1,0:T(8,128)S(1)}, s32[1,512]{1,0:T(1,128)S(1)}, s32[4]{0:T(128)S(1)}, /*index=5*/...) while((s32[]{:T(128)}, f32[1,6,512]{2,1,0:T(8,128)S(1)}, ...), condition=%wide.region_6.6_spmd.clone, body=%wide.region_3.5_spmd.clone.sunk | while | flops 214187008 | bytes 15110338 | solution.py:98
  260.6 26.4 %while.76 = (s32[]{:T(128)}, f32[1,512,6,64]{1,3,2,0:T(8,128)}, s32[4]{0:T(128)S(1)}, bf16[1,2048,384]{1,2,0:T(8,128)(2,1)}, s32[1,512]{1,0:T(1,128)S(1)}, /*ind...) while((s32[]{:T(128)}, f32[1,512,6,64]{1,3,2,0:T(8,128)}, ...), condition=%wide.region_8.8_spmd.clone, body=%wide.region_7.7_spmd.clone.sunk | while | flops 409600000 | bytes 4870345 | solution.py:119
  291.3 39.1 %while.75 = (s32[]{:T(128)}, f32[1,6,512]{2,1,0:T(8,128)S(1)}, f32[1,6,512]{2,1,0:T(8,128)S(1)}, s32[1,512]{1,0:T(1,128)S(1)}, s32[4]{0:T(128)S(1)}, /*index=5*/...) while((s32[]{:T(128)}, f32[1,6,512]{2,1,0:T(8,128)S(1)}, ...), condition=%wide.region_6.6_spmd.clone, body=%wide.region_3.5_spmd.clone.sunk | while | flops 214187008 | bytes 15110338 | solution.py:98
  331.1 26.6 %while.76 = (s32[]{:T(128)}, f32[1,512,6,64]{1,3,2,0:T(8,128)}, s32[4]{0:T(128)S(1)}, bf16[1,2048,384]{1,2,0:T(8,128)(2,1)}, s32[1,512]{1,0:T(1,128)S(1)}, /*ind...) while((s32[]{:T(128)}, f32[1,512,6,64]{1,3,2,0:T(8,128)}, ...), condition=%wide.region_8.8_spmd.clone, body=%wide.region_7.7_spmd.clone.sunk | while | flops 409600000 | bytes 4870345 | solution.py:119
  362.0 38.8 %while.75 = (s32[]{:T(128)}, f32[1,6,512]{2,1,0:T(8,128)S(1)}, f32[1,6,512]{2,1,0:T(8,128)S(1)}, s32[1,512]{1,0:T(1,128)S(1)}, s32[4]{0:T(128)S(1)}, /*index=5*/...) while((s32[]{:T(128)}, f32[1,6,512]{2,1,0:T(8,128)S(1)}, ...), condition=%wide.region_6.6_spmd.clone, body=%wide.region_3.5_spmd.clone.sunk | while | flops 214187008 | bytes 15110338 | solution.py:98
  401.5 26.3 %while.76 = (s32[]{:T(128)}, f32[1,512,6,64]{1,3,2,0:T(8,128)}, s32[4]{0:T(128)S(1)}, bf16[1,2048,384]{1,2,0:T(8,128)(2,1)}, s32[1,512]{1,0:T(1,128)S(1)}, /*ind...) while((s32[]{:T(128)}, f32[1,512,6,64]{1,3,2,0:T(8,128)}, ...), condition=%wide.region_8.8_spmd.clone, body=%wide.region_7.7_spmd.clone.sunk | while | flops 409600000 | bytes 4870345 | solution.py:119
  432.2 38.8 %while.75 = (s32[]{:T(128)}, f32[1,6,512]{2,1,0:T(8,128)S(1)}, f32[1,6,512]{2,1,0:T(8,128)S(1)}, s32[1,512]{1,0:T(1,128)S(1)}, s32[4]{0:T(128)S(1)}, /*index=5*/...) while((s32[]{:T(128)}, f32[1,6,512]{2,1,0:T(8,128)S(1)}, ...), condition=%wide.region_6.6_spmd.clone, body=%wide.region_3.5_spmd.clone.sunk | while | flops 214187008 | bytes 15110338 | solution.py:98
  471.7 26.3 %while.76 = (s32[]{:T(128)}, f32[1,512,6,64]{1,3,2,0:T(8,128)}, s32[4]{0:T(128)S(1)}, bf16[1,2048,384]{1,2,0:T(8,128)(2,1)}, s32[1,512]{1,0:T(1,128)S(1)}, /*ind...) while((s32[]{:T(128)}, f32[1,512,6,64]{1,3,2,0:T(8,128)}, ...), condition=%wide.region_8.8_spmd.clone, body=%wide.region_7.7_spmd.clone.sunk | while | flops 409600000 | bytes 4870345 | solution.py:119
  509.4 30.1 %copy.320 = bf16[1,2048,384]{2,0,1:T(2,128)(2,1)S(1)} copy(bf16[1,2048,384]{2,1,0:T(8,128)(2,1)S(1)} %bitcast.418) | data formatting | bytes 3145728 | tf_op jit(solution)/shard_map/convert_element_type | solution.py:280
  539.5 34.8 %reduce.12 = bf16[2048,384]{1,0:T(8,128)(2,1)} reduce(bf16[2048,1,384]{2,1,0:T(2,128)(2,1)S(1)} %bitcast.397, bf16[]{:T(256)} %broadcast.329), dimensions={1}, to_apply=%bitcast.271.reduce_sub_computation | reduce | bytes 3145730
  598.1 38.1 %multiply_convert_fusion.1 = (bf16[1024,3072]{1,0:T(8,128)(2,1)}, f32[1024,3072]{1,0:T(8,128)}, f32[1024,3072]{1,0:T(8,128)}) fusion(f32[3072]{0:T(1024)S(1)} %copy-done.49, bf16[768,3072]{1,0:T(8,128)(2,1)} %all-gather.15.cloned.1.call-done, f32[1024,768]{0,1:T(8,128)} %copy-done.12, f32[768]{0:T(1024)S(1)} %copy-done.51, f32[768]{0:T(1024)S(1)} %copy-done.41, ...), kind=kOutput, calls=%fused_computation.67 | convolution fusion | flops 5043388416 | bytes 39348224 | tf_op jit(solution)/shard_map/dot_general | solution.py:13
  651.9 18.1 convert_reduce_fusion
  670.1 11.5 multiply_reduce_fusion
  695.1 11.1 reduce.13
  740.3 479.1 %while.74 = (s32[]{:T(128)}, f32[1,2048,6,64]{1,3,2,0:T(8,128)}, bf16[4,1,512,384]{3,2,0,1:T(8,128)(2,1)}, bf16[4,1,512,384]{3,2,0,1:T(8,128)(2,1)}, s32[4]{0:T(...) while((s32[]{:T(128)}, f32[1,2048,6,64]{1,3,2,0:T(8,128)}, ...), condition=%wide.region_22.23_spmd.clone, body=%wide.region_19.22_spmd.clone.sunk | while | flops 1024000000 | bytes 62506448 | solution.py:187
  745.9 110.8 %while.77 = (s32[]{:T(128)}, f32[1,512,6,64]{1,3,2,0:T(8,128)}, f32[1,512,6,64]{1,3,2,0:T(8,128)}, f32[1,2048,6,64]{1,3,2,0:T(8,128)}, s32[4]{0:T(128)}, /*index...) while((s32[]{:T(128)}, f32[1,512,6,64]{1,3,2,0:T(8,128)}, ...), condition=%wide.region_21.21_spmd.clone, body=%wide.region_20.20_spmd.clone.sunk | while | flops 1024000000 | bytes 56996404 | solution.py:179
  865.8 110.6 %while.77 = (s32[]{:T(128)}, f32[1,512,6,64]{1,3,2,0:T(8,128)}, f32[1,512,6,64]{1,3,2,0:T(8,128)}, f32[1,2048,6,64]{1,3,2,0:T(8,128)}, s32[4]{0:T(128)}, /*index...) while((s32[]{:T(128)}, f32[1,512,6,64]{1,3,2,0:T(8,128)}, ...), condition=%wide.region_21.21_spmd.clone, body=%wide.region_20.20_spmd.clone.sunk | while | flops 1024000000 | bytes 56996404 | solution.py:179
  985.5 110.6 %while.77 = (s32[]{:T(128)}, f32[1,512,6,64]{1,3,2,0:T(8,128)}, f32[1,512,6,64]{1,3,2,0:T(8,128)}, f32[1,2048,6,64]{1,3,2,0:T(8,128)}, s32[4]{0:T(128)}, /*index...) while((s32[]{:T(128)}, f32[1,512,6,64]{1,3,2,0:T(8,128)}, ...), condition=%wide.region_21.21_spmd.clone, body=%wide.region_20.20_spmd.clone.sunk | while | flops 1024000000 | bytes 56996404 | solution.py:179
  1105.1 110.6 %while.77 = (s32[]{:T(128)}, f32[1,512,6,64]{1,3,2,0:T(8,128)}, f32[1,512,6,64]{1,3,2,0:T(8,128)}, f32[1,2048,6,64]{1,3,2,0:T(8,128)}, s32[4]{0:T(128)}, /*index...) while((s32[]{:T(128)}, f32[1,512,6,64]{1,3,2,0:T(8,128)}, ...), condition=%wide.region_21.21_spmd.clone, body=%wide.region_20.20_spmd.clone.sunk | while | flops 1024000000 | bytes 56996404 | solution.py:179
  1230.6 34.4 %reduce.15 = bf16[2048,384]{1,0:T(8,128)(2,1)} reduce(bf16[2048,1,384]{2,1,0:T(2,128)(2,1)S(1)} %bitcast.401, bf16[]{:T(256)} %broadcast.329), dimensions={1}, to_apply=%bitcast.224.reduce_sub_computation | reduce | bytes 3145730
  1286.0 28.4 %copy.318 = bf16[1,2048,384]{2,0,1:T(2,128)(2,1)} copy(bf16[1,2048,384]{2,1,0:T(8,128)(2,1)S(1)} %bitcast.435) | data formatting | bytes 3145728 | tf_op jit(solution)/shard_map/convert_element_type | solution.py:336
  1314.4 34.3 %reduce.16 = bf16[2048,384]{1,0:T(8,128)(2,1)S(1)} reduce(bf16[2048,1,384]{2,1,0:T(2,128)(2,1)} %bitcast.403, bf16[]{:T(256)} %broadcast.329), dimensions={1}, to_apply=%bitcast.269.reduce_sub_computation | reduce | bytes 3145730
  1372.1 28.4 %copy.319 = bf16[1,2048,384]{2,0,1:T(2,128)(2,1)} copy(bf16[1,2048,384]{2,1,0:T(8,128)(2,1)S(1)} %bitcast.434) | data formatting | bytes 3145728 | tf_op jit(solution)/shard_map/convert_element_type | solution.py:334
  1400.5 34.3 %reduce.14 = bf16[2048,384]{1,0:T(8,128)(2,1)S(1)} reduce(bf16[2048,1,384]{2,1,0:T(2,128)(2,1)} %bitcast.391, bf16[]{:T(256)} %broadcast.329), dimensions={1}, to_apply=%bitcast.270.reduce_sub_computation | reduce | bytes 3145730
  1482.9 40.2 %all-reduce.18 = (f32[768]{0:T(1024)S(1)}, f32[768]{0:T(1024)S(1)}, f32[768]{0:T(1024)S(1)}, f32[768]{0:T(1024)S(1)}, f32[768]{0:T(1024)S(1)}, /*index=5*/f32[30...) all-reduce(f32[768]{0:T(1024)S(1)} %reduce_sum.203, ...), channel_id=3, replica_groups=mesh['seq'=2,'shard'=16] {'seq','shard'}, use_global_device_ids=true, to_apply=%region_25.26.clone | all-reduce | flops 9216 | bytes 73728
  1540.3 52.1 %reduce-scatter.21.cloned.1.call-done = f32[24,768]{1,0:T(8,128)} async-done(((f32[768,768]{1,0:T(8,128)}), f32[24,768]{1,0:T(8,128)}) %reduce-scatter.21.cloned.1.call-update) | async-done | bytes 73744
  1592.4 141.2 %reduce-scatter.15.cloned.1.call-done = f32[24,3072]{1,0:T(8,128)} async-done(((f32[768,3072]{1,0:T(8,128)}), f32[24,3072]{1,0:T(8,128)}) %reduce-scatter.15.cloned.1.call-update) | async-done | bytes 294928 | tf_op jit(solution)/shard_map/reduce_scatter | solution.py:380
  1733.7 142.0 %reduce-scatter.17.cloned.1.call-done = f32[96,768]{1,0:T(8,128)} async-done(((f32[3072,768]{1,0:T(8,128)}), f32[96,768]{1,0:T(8,128)}) %reduce-scatter.17.cloned.1.call-update) | async-done | bytes 294928 | tf_op jit(solution)/shard_map/reduce_scatter | solution.py:382
  (1061 shorter events, 1042.8 us)
Async XLA Ops:
  7.2 61.3 %copy-start.24 = (bf16[1,1024,768]{2,1,0:T(8,128)(2,1)S(1)}, bf16[1,1024,768]{2,1,0:T(8,128)(2,1)}, u32[]{:S(2)}) copy-start(bf16[1,1024,768]{2,1,0:T(8,128)(2,1)} %param.45) | copy-start | bytes 4718596
  7.2 63.5 %all-gather.7.cloned.1.call-start = ((), (), s32[]{:S(2)}) async-start(), calls=%async_computation.14 | async-start | bytes 1216512 | tf_op jit(solution)/shard_map/all_gather | solution.py:236
  7.9 116.1 %all-gather.11.cloned.1.call-start = ((), (), s32[]{:S(2)}) async-start(), calls=%async_computation.16 | async-start | bytes 1216512 | tf_op jit(solution)/shard_map/all_gather | solution.py:238
  8.7 171.3 %all-gather.9.cloned.1.call-start = ((), (), s32[]{:S(2)}) async-start(), calls=%async_computation.15 | async-start | bytes 1216512 | tf_op jit(solution)/shard_map/all_gather | solution.py:237
  9.4 578.1 %all-gather.13.cloned.1.call-start = ((), (), s32[]{:S(2)}) async-start(), calls=%async_computation.17 | async-start | bytes 1216512 | tf_op jit(solution)/shard_map/all_gather | solution.py:239
  10.0 588.1 %all-gather.15.cloned.1.call-start = ((), (), s32[]{:S(2)}) async-start(), calls=%async_computation.18 | async-start | bytes 4866048 | tf_op jit(solution)/shard_map/all_gather | solution.py:240
  10.6 625.6 %all-gather.17.cloned.1.call-start = ((), (), s32[]{:S(2)}) async-start(), calls=%async_computation.19 | async-start | bytes 4866048 | tf_op jit(solution)/shard_map/all_gather | solution.py:241
  11.2 1529.1 %reduce-scatter.13.cloned.1.call-start = ((), (), s32[]{:S(2)}) async-start(), calls=%async_computation.20 | async-start | bytes 2433024 | tf_op jit(solution)/shard_map/reduce_scatter | solution.py:376
  106.1 18.0 copy-start.26
  158.5 21.5 %copy-start.27 = (bf16[1,1024,768]{2,1,0:T(8,128)(2,1)S(1)}, bf16[1,1024,768]{2,1,0:T(8,128)(2,1)}, u32[]{:S(2)}) copy-start(bf16[1,1024,768]{2,1,0:T(8,128)(2,1)} %param.28) | copy-start | bytes 4718596
  500.0 9.3 copy-start.2
  500.0 9.3 copy-start.19
  591.6 89.9 %copy-start.38 = (f32[1024]{0:T(1024)}, f32[1024]{0:T(1024)S(1)}, u32[]{:S(2)}) copy-start(f32[1024]{0:T(1024)S(1)} %broadcast_multiply_fusion.5) | copy-start | bytes 12292
  594.6 86.9 %copy-start.43 = (f32[1024]{0:T(1024)}, f32[1024]{0:T(1024)S(1)}, u32[]{:S(2)}) copy-start(f32[1024]{0:T(1024)S(1)} %add_rsqrt_fusion.1) | copy-start | bytes 12292
  598.0 38.2 %copy-start.13 = (f32[1024,768]{0,1:T(8,128)S(1)}, f32[1024,768]{0,1:T(8,128)}, u32[]{:S(2)}) copy-start(f32[1024,768]{0,1:T(8,128)} %copy-done.12) | copy-start | bytes 9437188
  598.0 38.2 %copy-start.53 = (f32[768]{0:T(1024)S(1)}, f32[768]{0:T(1024)}, u32[]{:S(2)}) copy-start(f32[768]{0:T(1024)} %convert_element_type.194) | copy-start | bytes 9220
  651.9 18.2 copy-start.35
  670.1 11.5 copy-start.14
  734.3 806.0 %reduce-scatter.19.cloned.1.call-start = ((), (), s32[]{:S(2)}) async-start(), calls=%async_computation.23 | async-start | bytes 2433024
  746.0 9.1 copy-start.20
  772.7 9.1 copy-start.20
  800.8 9.1 copy-start.20
  828.8 9.1 copy-start.20
  892.4 9.1 copy-start.20
  948.4 9.1 copy-start.20
  1068.1 9.1 copy-start.20
  1187.7 9.1 copy-start.20
  1285.9 254.3 %reduce-scatter.23.cloned.1.call-start = ((), (), s32[]{:S(2)}) async-start(), calls=%async_computation.25 | async-start | bytes 2433024
  1370.7 221.7 %reduce-scatter.21.cloned.1.call-start = ((), (), s32[]{:S(2)}) async-start(), calls=%async_computation.24 | async-start | bytes 2433024
  1456.7 276.9 %reduce-scatter.15.cloned.1.call-start = ((), (), s32[]{:S(2)}) async-start(), calls=%async_computation.21 | async-start | bytes 9732096 | tf_op jit(solution)/shard_map/reduce_scatter | solution.py:380
  1467.4 408.2 %reduce-scatter.17.cloned.1.call-start = ((), (), s32[]{:S(2)}) async-start(), calls=%async_computation.22 | async-start | bytes 9732096 | tf_op jit(solution)/shard_map/reduce_scatter | solution.py:382
  1480.7 47.0 %copy-start.30 = (bf16[1,1024,2,384]{1,3,2,0:T(8,128)(2,1)S(1)}, bf16[1,1024,2,384]{1,3,2,0:T(8,128)(2,1)}, u32[]{:S(2)}) copy-start(bf16[1,1024,2,384]{1,3,2,0:T(8,128)(2,1)} %copy.258) | copy-start | bytes 4718596
  (189 other events, 963.8 us)
Sparse Core Ops, SparseCore 0:
  10.9 56.9 all-gather.6
  70.8 53.1 all-gather.10
  126.9 52.9 all-gather.8
  182.7 53.0 all-gather.12
  238.6 62.4 all-gather.14
  303.8 62.3 all-gather.16
  734.4 97.8 reduce-scatter.12
  1286.1 97.6 reduce-scatter.18
  1389.7 98.1 reduce-scatter.22
  1494.4 97.9 reduce-scatter.20
  1598.9 134.7 reduce-scatter.14
  1741.0 134.6 reduce-scatter.16
where the time goes:
time: 1900 us; the launch traced here: 1880 us
  matrix products  568 us (30%)
  local copies, waits for them, and re-layouts  430 us (23%)
  waiting for transfers between devices  371 us (20%)
  other arithmetic  297 us (16%)
  blocking collectives  130 us (7%)
  loops' own time  71 us (4%)
    unnamed x8, other arithmetic  182 us
    reduce_scatter x1, waiting for transfers between devices, on_device(): lax.psum_scatter(d_w_down, ('seq', 'shard'), scatter_dimension=0, tiled=T...  142 us
    reduce_scatter x1, waiting for transfers between devices, on_device(): lax.psum_scatter(d_w_up, ('seq', 'shard'), scatter_dimension=0, tiled=True)  141 us
    dot_general x32, matrix products, masked_scores(): jnp.einsum('sqhd,skhd->shqk', query_blk, key_blk, preferred_element_type=...  120 us
    unnamed x161, local copies, waits for them, and re-layouts  101 us
    unnamed x2, blocking collectives  82.6 us
    dot_general x16, matrix products, query_step(): jnp.einsum('shqk,sqhd->skhd', attn_prob.astype(jnp.bfloat16), grad_blk, p...  80.9 us
    dynamic_slice x116, local copies, waits for them, and re-layouts, take_rows(): return lax.dynamic_slice_in_dim(array, index * size, size, 1)  76.2 us
  transfers between devices with their start and end apart: 12, of which 5 were waited for; matrix products, arithmetic and copies ran while one was open for 63% of the time, Pallas kernels for 0%

commit v1 on v0

v1 whole, which is shorter than its diff:
```python
import jax
import jax.numpy as jnp
from jax import lax
from jax.experimental import pallas as pl
from jax.experimental.pallas import tpu as pltpu
from jax.sharding import PartitionSpec as P

HEADS = 12
HEAD_DIM = 64
BLOCK = 256
LOW = 4
BF16 = jnp.bfloat16
F32 = jnp.float32
MASKED = -1e30


def dot(left, right, dims):
    return lax.dot_general(left, right, (dims, ((), ())), preferred_element_type=F32)


def nn(left, right):
    return dot(left, right, ((1,), (0,)))


def nt(left, right):
    return dot(left, right, ((1,), (1,)))


def tn(left, right):
    return dot(left, right, ((0,), (0,)))


def doc_tables(lengths, count):
    ends = jnp.cumsum(lengths)
    starts = ends - lengths
    docs = lengths.shape[0]
    place = jnp.arange(count, dtype=jnp.int32)
    inside = (place[:, None] >= starts[None, :]) & (place[:, None] < ends[None, :])
    inside_t = (place[None, :] >= starts[:, None]) & (place[None, :] < ends[:, None])
    query_rows = jnp.pad(inside_t.astype(BF16), ((0, HEAD_DIM - docs), (0, 0)))
    penalty = jnp.where(inside, 0.0, MASKED).astype(BF16)
    half = jnp.concatenate(
        [penalty, jnp.ones((count, 3), BF16), jnp.zeros((count, HEAD_DIM - docs - 3), BF16)], 1
    )
    key_cols = jnp.concatenate([half, half], 1)
    first = jnp.arange(count // BLOCK, dtype=jnp.int32) * BLOCK
    last = first + BLOCK - 1
    begin = jnp.max(jnp.where(starts[None, :] <= first[:, None], starts[None, :], 0), 1)
    end = jnp.min(jnp.where(ends[None, :] > last[:, None], ends[None, :], count), 1)
    return (
        (begin // BLOCK).astype(jnp.int32),
        ((end + BLOCK - 1) // BLOCK).astype(jnp.int32),
        query_rows,
        key_cols,
    )


def join(part, extra, head):
    return jnp.concatenate([part, extra] if head % 2 == 0 else [extra, part], 0)


def fill_pairs(out, source, extra_of, count, heads):
    def step(index, _):
        rows = pl.ds(pl.multiple_of(index * BLOCK, BLOCK), BLOCK)
        lane = lax.broadcasted_iota(jnp.int32, (BLOCK, 128), 1)
        extra = extra_of(rows)
        for head in range(0, heads, 2):
            pair = source[rows, 64 * head : 64 * head + 128]
            out[head, rows] = jnp.where(lane < 64, pair, extra)
            out[head + 1, rows] = jnp.where(lane < 64, extra, pair)
        return 0

    lax.fori_loop(0, count // BLOCK, step, 0)


def attend_kernel(
    lo, hi, query_t, keys, values_t, query_rows, key_cols, out_t, log_sum, keys_ext, total_t, stats
):
    count = keys.shape[0]
    heads = query_t.shape[0] // HEAD_DIM
    block = pl.program_id(0)

    @pl.when(block == 0)
    def _():
        fill_pairs(keys_ext, keys, lambda rows: key_cols[rows, :], count, heads)

    extra = query_rows[...]
    query_ext = [join(query_t[64 * h : 64 * h + 64, :], extra, h) for h in range(heads)]
    total_t[...] = jnp.zeros_like(total_t)
    stats[0] = jnp.full(stats.shape[1:], MASKED, F32)
    stats[1] = jnp.zeros(stats.shape[1:], F32)

    def step(index, _):
        rows = pl.ds(pl.multiple_of(index * BLOCK, BLOCK), BLOCK)
        scores = [nn(keys_ext[h, rows, :], query_ext[h]) for h in range(heads)]
        for h in range(heads):
            top = stats[0, h : h + 1, :]
            new_top = jnp.maximum(top, jnp.max(scores[h], axis=0, keepdims=True))
            prob = jnp.exp(scores[h] - new_top)
            keep = jnp.exp(top - new_top)
            stats[1, h : h + 1, :] = stats[1, h : h + 1, :] * keep + jnp.sum(
                prob, axis=0, keepdims=True
            )
            stats[0, h : h + 1, :] = new_top
            total_t[h] = total_t[h] * keep + nn(
                values_t[64 * h : 64 * h + 64, rows], prob.astype(BF16)
            )
        return 0

    lax.fori_loop(lo[block], hi[block], step, 0)
    for h in range(heads):
        norm = stats[1, h : h + 1, :]
        out_t[64 * h : 64 * h + 64, :] = total_t[h] * (1.0 / norm)
        log_sum[h : h + 1, :] = stats[0, h : h + 1, :] + jnp.log(norm)


def attend(lo, hi, query_t, keys, values_t, query_rows, key_cols):
    count, width = keys.shape
    heads = width // HEAD_DIM
    whole = lambda shape: pl.BlockSpec(shape, lambda b, *_: (0, 0))
    column = lambda rows: pl.BlockSpec((rows, BLOCK), lambda b, *_: (0, b))
    return pl.pallas_call(
        attend_kernel,
        grid_spec=pltpu.PrefetchScalarGridSpec(
            num_scalar_prefetch=2,
            grid=(count // BLOCK,),
            in_specs=[
                column(width),
                whole((count, width)),
                whole((width, count)),
                column(HEAD_DIM),
                whole((count, 128)),
            ],
            out_specs=[column(width), column(8)],
            scratch_shapes=[
                pltpu.VMEM((heads, count, 128), BF16),
                pltpu.VMEM((heads, HEAD_DIM, BLOCK), F32),
                pltpu.VMEM((2, 8, BLOCK), F32),
            ],
        ),
        out_shape=[
            jax.ShapeDtypeStruct((width, count), F32),
            jax.ShapeDtypeStruct((8, count), F32),
        ],
        name="attend",
        cost_estimate=pl.CostEstimate(
            flops=4 * count * count * width, bytes_accessed=12 * count * width, transcendentals=0
        ),
    )(lo, hi, query_t, keys, values_t, query_rows, key_cols)


def three_parts(value):
    high = value.astype(BF16).astype(F32)
    middle = (value - high).astype(BF16).astype(F32)
    return (high, middle, value - high - middle)


def attend_back_kernel(
    lo, hi, query_t, keys, values, grad, out_t, log_sum, query_rows, key_cols,
    grad_all, keys_ext, values_ext, keys_t, grad_keys, grad_values,
):
    count, width = keys.shape
    heads = width // HEAD_DIM
    block = pl.program_id(0)

    @pl.when(block == 0)
    def _():
        fill_pairs(keys_ext, keys, lambda rows: key_cols[rows, :], count, heads)
        fill_pairs(values_ext, values, lambda rows: jnp.ones((BLOCK, 128), BF16), count, heads)

        def turn(index, _):
            rows = pl.ds(pl.multiple_of(index * BLOCK, BLOCK), BLOCK)
            keys_t[:, rows] = keys[rows, :].T
            return 0

        lax.fori_loop(0, count // BLOCK, turn, 0)
        grad_keys[...] = jnp.zeros_like(grad_keys)
        grad_values[...] = jnp.zeros_like(grad_values)

    row = lax.broadcasted_iota(jnp.int32, (HEAD_DIM, BLOCK), 0)
    extra = query_rows[...].astype(F32)
    grad_blk = grad[...]
    grad_t = grad_blk.T
    query_blk = query_t[...].T
    query_ext, grad_ext, query_own, grad_own = [], [], [], []
    for h in range(heads):
        span = slice(64 * h, 64 * h + 64)
        a, b, c = three_parts(-log_sum[h : h + 1, :])
        rows = jnp.where(row == 8, a, jnp.where(row == 9, b, jnp.where(row == 10, c, extra)))
        query_ext.append(join(query_t[span, :], rows.astype(BF16), h))
        delta = jnp.sum(grad_t[span, :].astype(F32) * out_t[span, :], axis=0, keepdims=True)
        a, b, c = three_parts(-delta)
        rows = jnp.where(row == 0, a, jnp.where(row == 1, b, jnp.where(row == 2, c, 0.0)))
        grad_ext.append(join(grad_t[span, :], rows.astype(BF16), h))
        query_own.append(query_blk[:, span])
        grad_own.append(grad_blk[:, span])

    def step(index, carry):
        rows = pl.ds(pl.multiple_of(index * BLOCK, BLOCK), BLOCK)
        scores = [nn(keys_ext[h, rows, :], query_ext[h]) for h in range(heads)]
        lifts = [nn(values_ext[h, rows, :], grad_ext[h]) for h in range(heads)]
        out = []
        for h in range(heads):
            prob = jnp.exp(scores[h])
            grad_scores = (prob * lifts[h]).astype(BF16)
            grad_values[h, rows, :] += nn(prob.astype(BF16), grad_own[h])
            grad_keys[h, rows, :] += nn(grad_scores, query_own[h])
            out.append(carry[h] + nn(keys_t[64 * h : 64 * h + 64, rows], grad_scores))
        return tuple(out)

    zero = jnp.zeros((HEAD_DIM, BLOCK), F32)
    grads = lax.fori_loop(lo[block], hi[block], step, (zero,) * heads)
    own = pl.ds(pl.multiple_of(block * BLOCK, BLOCK), BLOCK)
    for h in range(0, heads, 2):
        pair = jnp.concatenate([grads[h], grads[h + 1]], 0) * (HEAD_DIM**-0.5)
        grad_all[own, 64 * h : 64 * h + 128] = pair.T.astype(BF16)

    @pl.when(block == pl.num_programs(0) - 1)
    def _():
        def finish(index, _):
            rows = pl.ds(pl.multiple_of(index * BLOCK, BLOCK), BLOCK)
            for h in range(0, heads, 2):
                for place, held in ((width, grad_keys), (2 * width, grad_values)):
                    pair = jnp.concatenate([held[h, rows, :], held[h + 1, rows, :]], 1)
                    grad_all[rows, place + 64 * h : place + 64 * h + 128] = pair.astype(BF16)
            return 0

        lax.fori_loop(0, count // BLOCK, finish, 0)


def attend_back(lo, hi, query_t, keys, values, grad, out_t, log_sum, query_rows, key_cols):
    count, width = keys.shape
    heads = width // HEAD_DIM
    whole = lambda shape: pl.BlockSpec(shape, lambda b, *_: (0, 0))
    column = lambda rows: pl.BlockSpec((rows, BLOCK), lambda b, *_: (0, b))
    return pl.pallas_call(
        attend_back_kernel,
        grid_spec=pltpu.PrefetchScalarGridSpec(
            num_scalar_prefetch=2,
            grid=(count // BLOCK,),
            in_specs=[
                column(width),
                whole((count, width)),
                whole((count, width)),
                pl.BlockSpec((BLOCK, width), lambda b, *_: (b, 0)),
                column(width),
                column(8),
                column(HEAD_DIM),
                whole((count, 128)),
            ],
            out_specs=whole((count, 3 * width)),
            scratch_shapes=[
                pltpu.VMEM((heads, count, 128), BF16),
                pltpu.VMEM((heads, count, 128), BF16),
                pltpu.VMEM((width, count), BF16),
                pltpu.VMEM((heads, count, HEAD_DIM), F32),
                pltpu.VMEM((heads, count, HEAD_DIM), F32),
            ],
        ),
        out_shape=jax.ShapeDtypeStruct((count, 3 * width), BF16),
        name="attend_back",
        cost_estimate=pl.CostEstimate(
            flops=10 * count * count * width, bytes_accessed=20 * count * width, transcendentals=0
        ),
    )(lo, hi, query_t, keys, values, grad, out_t, log_sum, query_rows, key_cols)


def swap(array):
    return lax.ppermute(array, "seq", [(0, 1), (1, 0)])


def low_hop(array, mask):
    size = lax.axis_size("shard")
    return lax.ppermute(
        array, "shard", [(a, a // LOW * LOW + ((a % LOW) ^ mask)) for a in range(size)]
    )


def high_hop(array, step):
    size = lax.axis_size("shard")
    return lax.ppermute(
        array,
        "shard",
        [(a, (a // LOW + step) % (size // LOW) * LOW + a % LOW) for a in range(size)],
    )


def put(whole, part, index):
    return lax.dynamic_update_slice_in_dim(whole, part[None], index, 0)


def pick(whole, index, axis=0):
    return lax.dynamic_index_in_dim(whole, index, axis, keepdims=False)


def gather_shards(block):
    high = lax.axis_size("shard") // LOW
    index = lax.axis_index("shard")
    mine_high, mine_low = index // LOW, index % LOW
    column = put(jnp.zeros((high, *block.shape), block.dtype), block, mine_high)
    for step in range(1, high):
        column = put(column, high_hop(block, step), (mine_high - step) % high)
    whole = put(jnp.zeros((LOW, *column.shape), block.dtype), column, mine_low)
    for mask in range(1, LOW):
        whole = put(whole, low_hop(column, mask), mine_low ^ mask)
    return whole


def scatter_low(take, mine_low):
    received = [low_hop(take(mine_low ^ mask), mask) for mask in range(1, LOW)]
    total = take(mine_low).astype(F32)
    for part in received:
        total = total + part.astype(F32)
    return total


def scatter_high(column):
    high = column.shape[0]
    mine = lax.axis_index("shard") // LOW
    low = column.astype(BF16)
    received = [high_hop(pick(low, (mine + step) % high), step) for step in range(1, high)]
    total = pick(column, mine)
    for part in received:
        total = total + part.astype(F32)
    return total


def norm(hidden):
    centred = hidden - jnp.mean(hidden, axis=-1, keepdims=True)
    factor = lax.rsqrt(jnp.mean(centred * centred, axis=-1, keepdims=True) + 1e-12)
    return (centred * factor, factor)


def norm_back(grad, normed, factor, gain):
    scaled = grad * gain
    inner = (
        scaled
        - jnp.mean(scaled, axis=-1, keepdims=True)
        - normed * jnp.mean(scaled * normed, axis=-1, keepdims=True)
    )
    return factor * inner


def on_device(
    tokens, lengths, query_weight, query_bias, key_weight, value_weight, value_bias,
    output_weight, output_bias, first_gain, first_shift, up_weight, up_bias, down_weight,
    down_bias, second_gain, second_shift, cotangent,
):
    _, half_len, width = tokens.shape
    count = 2 * half_len
    half = width // 2
    hidden = up_weight.shape[1]
    rows = query_weight.shape[0]
    wide = hidden // width
    shards = lax.axis_size("shard")
    high = shards // LOW
    devices = 2 * shards
    me = lax.axis_index("seq")
    index = lax.axis_index("shard")
    mine_low = index % LOW
    own_tokens = tokens[0]

    both = jnp.concatenate([query_weight, key_weight, value_weight], 0).reshape(3, rows, 2, half)
    kept = pick(both, me, 2)
    got = swap(pick(both, 1 - me, 2))
    pair = put(put(jnp.zeros((2, 3, rows, half), BF16), kept, me), got, 1 - me)
    small = jnp.concatenate([query_bias, value_bias])
    small = jnp.pad(small, (0, half - small.shape[0])).reshape(1, 1, 1, half)
    block = jnp.concatenate(
        [pair.reshape(1, 1, 6 * rows, half), jnp.pad(small, ((0, 0), (0, 0), (0, 7), (0, 0)))], 2
    )[0, 0]
    gathered = gather_shards(block)
    weights = gathered[:, :, : 6 * rows].reshape(LOW, high, 2, 3, rows, half)
    weights = weights.transpose(3, 2, 1, 0, 4, 5).reshape(3, width, half)
    w_query, w_key, w_value = weights[0], weights[1], weights[2]
    biases = gathered[:, :, 6 * rows, : 2 * rows].reshape(LOW, high, 2, rows)
    biases = biases.transpose(2, 1, 0, 3).reshape(2, half).astype(F32)
    b_query, b_value = biases[0], biases[1]

    vectors = jnp.concatenate(
        [output_bias, first_gain, first_shift, down_bias, second_gain, second_shift, up_bias]
    )
    line = jnp.pad(vectors, (0, width - vectors.shape[0])).reshape(1, width)
    pack = jnp.concatenate(
        [
            output_weight,
            up_weight.reshape(rows, wide, width).transpose(1, 0, 2).reshape(wide * rows, width),
            down_weight,
            jnp.pad(line, ((0, 7), (0, 0))),
        ],
        0,
    )
    rest = lax.all_gather(pack, ("seq", "shard"), axis=0, tiled=False)

    other_tokens = swap(own_tokens)
    both_tokens = put(put(jnp.zeros((2, half_len, width), BF16), own_tokens, me), other_tokens, 1 - me)
    x = both_tokens.reshape(count, width)

    scale = HEAD_DIM**-0.5
    query_t = (
        (dot(w_query, x, ((0,), (1,))) + b_query[:, None]).astype(BF16) * jnp.asarray(scale, BF16)
    )
    keys = nn(x, w_key).astype(BF16)
    values_t = (dot(w_value, x, ((0,), (1,))) + b_value[:, None]).astype(BF16)
    values = (nn(x, w_value) + b_value).astype(BF16)

    lo, hi, query_rows, key_cols = doc_tables(lengths[0], count)
    out_t, log_sum = attend(lo, hi, query_t, keys, values_t, query_rows, key_cols)
    low_t = out_t.astype(BF16).reshape(half, 2, half_len)
    mixed_t = put(
        put(jnp.zeros((2, half, half_len), BF16), pick(low_t, me, 1), me),
        swap(pick(low_t, 1 - me, 1)),
        1 - me,
    ).reshape(width, half_len)

    w_out = rest[:, :rows].reshape(width, width)
    w_up = (
        rest[:, rows : rows + wide * rows]
        .reshape(devices, wide, rows, width)
        .transpose(0, 2, 1, 3)
        .reshape(width, hidden)
    )
    w_down = rest[:, rows + wide * rows : rows + 2 * wide * rows].reshape(hidden, width)
    lines = rest[:, rows + 2 * wide * rows]
    b_out, gain_one, shift_one, b_down, gain_two, shift_two = (
        lines[:, : 6 * rows].reshape(devices, 6, rows).transpose(1, 0, 2).reshape(6, width).astype(F32)
    )
    b_up = lines[:, 6 * rows : 6 * rows + wide * rows].reshape(hidden).astype(F32)

    branch = tn(mixed_t, w_out) + b_out
    normed_one, factor_one = norm(own_tokens.astype(F32) + branch)
    first = normed_one * gain_one + shift_one
    first_low = first.astype(BF16)
    preact = nn(first_low, w_up) + b_up
    cdf = 0.5 * (1.0 + lax.erf(preact * (0.5**0.5)))
    density = jnp.exp(-0.5 * preact * preact) * 0.3989422804014327
    activated = (preact * cdf).astype(BF16)
    slope = (cdf + preact * density).astype(BF16)
    second_in = first + nn(activated, w_down) + b_down
    normed_two, factor_two = norm(second_in)
    output = (normed_two * gain_two + shift_two).astype(BF16)

    grad_y = cotangent[0].astype(F32)
    d_gain_two = jnp.sum(grad_y * normed_two, axis=0)
    d_shift_two = jnp.sum(grad_y, axis=0)
    g_second = norm_back(grad_y, normed_two, factor_two, gain_two)
    g_down = g_second.astype(BF16)
    d_down = tn(activated, g_down).astype(BF16)
    d_b_down = jnp.sum(g_down.astype(F32), axis=0)
    g_pre = (nt(g_down, w_down) * slope.astype(F32)).astype(BF16)
    d_up = tn(first_low, g_pre).astype(BF16)
    d_b_up = jnp.sum(g_pre.astype(F32), axis=0)
    g_first = g_second + nt(g_pre, w_up)
    d_gain_one = jnp.sum(g_first * normed_one, axis=0)
    d_shift_one = jnp.sum(g_first, axis=0)
    g_res = norm_back(g_first, normed_one, factor_one, gain_one)
    g_branch = g_res.astype(BF16)
    d_out = nn(mixed_t, g_branch).astype(BF16)
    d_b_out = jnp.sum(g_branch.astype(F32), axis=0)
    g_mixed = nt(g_branch, w_out).astype(BF16).reshape(half_len, 2, half)
    grad_heads = put(
        put(jnp.zeros((2, half_len, half), BF16), pick(g_mixed, me, 1), me),
        swap(pick(g_mixed, 1 - me, 1)),
        1 - me,
    ).reshape(count, half)

    parts = [
        d_out.reshape(2, high, LOW, 1, rows, width),
        d_up.reshape(2, high, LOW, rows, wide, width).transpose(0, 1, 2, 4, 3, 5),
        d_down.reshape(2, high, LOW, wide, rows, width),
    ]
    grads = jnp.stack([d_b_out, d_gain_one, d_shift_one, d_b_down, d_gain_two, d_shift_two])
    grads = grads.reshape(6, devices, rows).transpose(1, 0, 2).reshape(devices, 6 * rows)
    grads = jnp.concatenate([grads, d_b_up.reshape(devices, wide * rows)], 1)
    grads = jnp.pad(grads, ((0, 0), (0, width - grads.shape[1]))).astype(BF16)
    grads = jnp.pad(grads.reshape(2, high, LOW, 1, 1, width), ((0, 0),) * 4 + ((0, rows - 1), (0, 0)))
    packed = jnp.concatenate([*parts, grads], 3)
    chip = pick(packed, me).astype(F32) + swap(pick(packed, 1 - me)).astype(F32)
    chip = chip.astype(BF16)
    column = scatter_low(lambda low: pick(chip, low, 1), mine_low)
    owned = scatter_high(column)

    grad_qkv = attend_back(
        lo, hi, query_t, keys, values, grad_heads, out_t, log_sum, query_rows, key_cols
    )
    d_qkv = tn(x, grad_qkv)
    d_bias = jnp.sum(grad_qkv.astype(F32), axis=0)
    d_bias = jnp.stack([d_bias[:half], d_bias[2 * half :]])

    terms = d_qkv.astype(BF16).reshape(2, high, LOW, rows, 3 * half)
    lines = d_bias.reshape(2, high, LOW, rows).transpose(1, 2, 0, 3).reshape(high, LOW, 2 * rows)
    lines = jnp.pad(lines, ((0, 0), (0, 0), (0, 3 * half - 2 * rows))).astype(BF16)
    lines = jnp.pad(lines.reshape(high, LOW, 1, 3 * half), ((0, 0), (0, 0), (0, 7), (0, 0)))
    terms = jnp.concatenate(
        [terms.transpose(1, 2, 0, 3, 4).reshape(high, LOW, 2 * rows, 3 * half), lines], 2
    )
    own_qkv = scatter_high(scatter_low(lambda low: pick(terms, low, 1), mine_low))
    r_biases = own_qkv[2 * rows, : 2 * rows].reshape(2, rows)
    two = own_qkv[: 2 * rows].reshape(2, rows, 3, half)
    mine, theirs = pick(two, me), swap(pick(two, 1 - me))
    r_qkv = put(put(jnp.zeros((2, rows, 3, half), F32), mine, me), theirs, 1 - me)
    r_qkv = r_qkv.transpose(2, 1, 0, 3).reshape(3, rows, width)

    w_all = jnp.concatenate([w_query, w_key, w_value], 1)
    back = nt(grad_qkv, w_all).reshape(2, half_len, width)
    grad_tokens = g_res + pick(back, me) + swap(pick(back, 1 - me))

    r_out = owned[0]
    r_up = owned[1 : 1 + wide].transpose(1, 0, 2).reshape(rows, hidden)
    r_down = owned[1 + wide : 1 + 2 * wide].reshape(wide * rows, width)
    r_line = owned[1 + 2 * wide, 0]
    r_vec = r_line[: 6 * rows].reshape(6, rows)
    r_b_up = r_line[6 * rows : 6 * rows + wide * rows]
    return (
        output[None], grad_tokens[None],
        r_qkv[0], r_biases[0], r_qkv[1], r_qkv[2], r_biases[1],
        r_out, r_vec[0], r_vec[1], r_vec[2], r_up, r_b_up, r_down, r_vec[3], r_vec[4], r_vec[5],
    )


def solution(mesh):
    rows = P(("seq", "shard"), None)
    line = P(("seq", "shard"))
    data = P("shard", "seq", None)
    return jax.shard_map(
        on_device,
        mesh=mesh,
        in_specs=(
            data, P("shard", None), rows, line, rows, rows, line, rows, line, line, line,
            rows, line, rows, line, line, line, data,
        ),
        out_specs=(
            data, data, rows, line, rows, rows, line, rows, line, line, line, rows, line, rows,
            line, line, line,
        ),
        check_vma=False,
    )
```

time: 1900 us -> 492 us (0.26)
  the two profiles are of different devices: /device:TPU:0 before, /device:TPU:10 now
where the time goes in v1:
time: 492 us; the launch traced here: 487 us
  local copies, waits for them, and re-layouts  113 us (23%)
  waiting for transfers between devices  113 us (23%)
  matrix products  91.4 us (19%)
  Pallas kernels  69.1 us (14%)
  other arithmetic  44.7 us (9%)
  starting transfers between devices  39.7 us (8%)
  between operations  15.5 us (3%)
    dot_general x15, matrix products, dot(): lax.dot_general(left, right, (dims, ((), ())), preferred_element_type=F32)  91.4 us
    ppermute x9, waiting for transfers between devices, low_hop(): lax.ppermute(array, 'shard', [(a, a // LOW * LOW + (a % LOW ^ mask)) for...  72.8 us
    pallas_call x1, Pallas kernels, attend_back(): pl.pallas_call(attend_back_kernel, grid_spec=pltpu.PrefetchScalarGridSpec...  41.7 us
    ppermute x9, waiting for transfers between devices, high_hop(): lax.ppermute(array, 'shard', [(a, (a // LOW + step) % (size // LOW) * LOW...  40.5 us
    unnamed x90, local copies, waits for them, and re-layouts  29 us
    pallas_call x1, Pallas kernels, attend(): pl.pallas_call(attend_kernel, grid_spec=pltpu.PrefetchScalarGridSpec(num_...  27.4 us
    ppermute x9, starting transfers between devices, low_hop(): lax.ppermute(array, 'shard', [(a, a // LOW * LOW + (a % LOW ^ mask)) for...  20 us
    ppermute x9, starting transfers between devices, high_hop(): lax.ppermute(array, 'shard', [(a, (a // LOW + step) % (size // LOW) * LOW...  18.4 us
  transfers between devices with their start and end apart: 26, of which 12 were waited for; matrix products, arithmetic and copies ran while one was open for 24% of the time, Pallas kernels for 14%

profile of v1, /device:TPU:10, one launch (start us, length us, event | category | flops | bytes accessed | tf_op | source)
XLA Modules:
  0.0 486.8 jit_solution(18438423703410953353)
XLA Ops:
  8.3 4.8 concatenate.41
  28.4 11.0 %collective-permute-done.2 = bf16[152,384]{1,0:T(8,128)(2,1)S(1)} collective-permute-done((bf16[152,384]{1,0:T(8,128)(2,1)S(1)}, bf16[152,384]{1,0:T(8,128)(2,1)S(1)}, u32[]{:S(2)}, u32[]{:S(2)}) %collective-permute-start.2) | collective-permute-done | bytes 116768 | tf_op jit(solution)/shard_map/ppermute | solution.py:281
  45.7 13.9 %collective-permute-done.4 = bf16[4,152,384]{2,1,0:T(8,128)(2,1)S(1)} collective-permute-done((bf16[4,152,384]{2,1,0:T(8,128)(2,1)S(1)}, bf16[4,152,384]{2,1,0:T(8,128)(2,1)S(1)}, u32[]{:S(2)}, u32[]{:S(2)}) %collective-permute-start.4) | collective-permute-done | bytes 466976 | tf_op jit(solution)/shard_map/ppermute | solution.py:274
  60.9 13.6 %collective-permute-done.6 = bf16[4,152,384]{2,1,0:T(8,128)(2,1)S(1)} collective-permute-done((bf16[4,152,384]{2,1,0:T(8,128)(2,1)S(1)}, bf16[4,152,384]{2,1,0:T(8,128)(2,1)S(1)}, u32[]{:S(2)}, u32[]{:S(2)}) %collective-permute-start.6) | collective-permute-done | bytes 466976 | tf_op jit(solution)/shard_map/ppermute | solution.py:274
  81.6 5.0 %convolution_convert_fusion.3.keys = bf16[2048,384]{1,0:T(8,128)(2,1)} fusion(bf16[2048,768]{1,0:T(8,128)(2,1)} %bitcast.258, bf16[768,384]{1,0:T(8,128)(2,1)S(1)} %bitcast.281), kind=kOutput, calls=%fused_computation.50 | convolution fusion | flops 1208745984 | bytes 5308416 | tf_op jit(solution)/shard_map/dot_general | solution.py:18
  92.0 27.4 %attend.1 = (f32[384,2048]{1,0:T(8,128)}, f32[8,2048]{1,0:T(8,128)}) custom-call(s32[8]{0:T(128)} %and_select_fusion.1.lo, s32[8]{0:T(128)} %and_select_fusion.hi, bf16[384,2048]{1,0:T(8,128)(2,1)} %fusion.21.query_t, bf16[2048,384]{1,0:T(8,128)(2,1)} %convolution_convert_fusion.3.keys, bf16[384,2048]{1,0:T(8,128)(2,1)} %add_convert_fusion.2.values_t, ...), custom_call_target="tpu_custom_call" | custom-call | flops 6442450944 | bytes 9437184 | tf_op jit(solution)/shard_map/attend/pallas_call | solution.py:122
  122.7 4.4 constant_dynamic-slice_fusion.6
  136.1 8.0 %fusion.65 = (bf16[32,96,768]{2,1,0:T(8,128)(2,1)}, bf16[32,96,768]{2,1,0:T(8,128)(2,1)}) fusion(bf16[32,224,768]{2,1,0:T(8,128)(2,1)} %bitcast.244), kind=kLoop, calls=%fused_computation.197 | loop fusion | bytes 18874368 | tf_op jit(solution)/shard_map/slice | solution.py:423
  144.5 3.8 fusion.72
  149.0 5.0 %copy.231 = bf16[32,4,24,768]{3,1,2,0:T(4,128)(2,1)S(1)} copy(bf16[32,4,24,768]{3,2,1,0:T(8,128)(2,1)} %bitcast.241) | data formatting | bytes 9437184 | tf_op jit(solution)/shard_map/reshape | solution.py:419
  157.5 11.7 %multiply_convert_fusion.1 = (bf16[1024,3072]{1,0:T(8,128)(2,1)S(1)}, f32[1024,3072]{1,0:T(8,128)}) fusion(f32[3072]{0:T(1024)S(1)} %reshape.344, bf16[768,3072]{1,0:T(8,128)(2,1)} %bitcast.250, f32[1024,768]{0,1:T(8,128)S(1)} %get-tuple-element.190, f32[768]{0:T(1024)S(1)} %add.338, f32[768]{0:T(1024)S(1)} %mul.154, f32[1024]{0:T(1024)S(1)} %add_rsqrt_fusion.1, ...), kind=kOutput, calls=%fused_computation.9 | convolution fusion | flops 4854644736 | bytes 26765312 | tf_op jit(solution)/shard_map/dot_general | solution.py:18
  169.3 10.3 %fusion.73 = (f32[1024]{0:T(1024)S(1)}, f32[1024,768]{0,1:T(8,128)S(1)}) fusion(f32[768]{0:T(1024)S(1)} %add.346, bf16[1024,3072]{1,0:T(8,128)(2,1)S(1)} %get-tuple-element.191, bf16[3072,768]{1,0:T(8,128)(2,1)} %bitcast.254, f32[768]{0:T(1024)S(1)} %add.338, f32[768]{0:T(1024)S(1)} %mul.154, f32[1024]{0:T(1024)S(1)} %add_rsqrt_fusion.1, ...), kind=kOutput, calls=%fused_computation.205 | convolution fusion | flops 4837342208 | bytes 17323008 | tf_op jit(solution)/shard_map/dot_general | solution.py:18
  185.4 12.6 %fusion.74 = (bf16[3072]{0:T(1024)(128)(2,1)S(1)}, bf16[1024,3072]{1,0:T(8,128)(2,1)S(1)}) fusion(f32[1024,3072]{1,0:T(8,128)} %get-tuple-element.192, f32[3072]{0:T(1024)S(1)} %reshape.344, bf16[1024,768]{0,1:T(8,128)(2,1)S(1)} %get-tuple-element.133, bf16[3072,768]{1,0:T(8,128)(2,1)} %bitcast.255), kind=kOutput, calls=%fused_computation.206 | convolution fusion | flops 4875875328 | bytes 25184256 | tf_op jit(solution)/shard_map/dot_general | solution.py:18
  198.0 6.6 %multiply_reduce_fusion = (bf16[768]{0:T(1024)(128)(2,1)S(1)}, f32[1024]{0:T(1024)S(1)}, f32[1024]{0:T(1024)S(1)}, bf16[768]{0:T(1024)(128)(2,1)S(1)}, f32[1024,768]{0,1:T(8,128)S(1)}) fusion(f32[1024,768]{0,1:T(8,128)S(1)} %copy-done.4, f32[1024]{0:T(1024)S(1)} %add_rsqrt_fusion.1, f32[1024]{0:T(1024)S(1)} %broadcast_multiply_fusion.5, f32[768]{0:T(1024)S(1)} %mul.154, ...), kind=kOutput, calls=%fused_computation.33 | convolution fusion | flops 4845989888 | bytes 22062080 | tf_op jit(solution)/shard_map/dot_general | solution.py:18
  204.6 7.2 %convolution_convert_fusion.1 = bf16[768,3072]{1,0:T(8,128)(2,1)} fusion(bf16[1024,3072]{1,0:T(8,128)(2,1)S(1)} %get-tuple-element.197, f32[1024,768]{0,1:T(8,128)S(1)} %copy-done.4, f32[768]{0:T(1024)S(1)} %add.338, f32[768]{0:T(1024)S(1)} %mul.154, f32[1024]{0:T(1024)S(1)} %add_rsqrt_fusion.1, f32[1024]{0:T(1024)S(1)} %broadcast_multiply_fusion.5), kind=kOutput, calls=%fused_computation.16 | convolution fusion | flops 4838129664 | bytes 14170112 | tf_op jit(solution)/shard_map/dot_general | solution.py:18
  211.8 9.9 %convolution_convert_fusion = bf16[3072,768]{1,0:T(8,128)(2,1)} fusion(bf16[1024,3072]{1,0:T(8,128)(2,1)} %copy-done.31, bf16[1024,768]{0,1:T(8,128)(2,1)S(1)} %get-tuple-element.133), kind=kOutput, calls=%fused_computation.15 | convolution fusion | flops 4834197504 | bytes 12582912 | tf_op jit(solution)/shard_map/dot_general | solution.py:18
  227.0 9.7 %reshape.337 = bf16[2,4,4,24,4,768]{5,4,3,2,1,0:T(4,128)(2,1)} reshape(bf16[768,3072]{1,0:T(8,128)(2,1)} %convolution_convert_fusion.1) | data formatting | bytes 9437184 | tf_op jit(solution)/shard_map/reshape | solution.py:469
  236.8 5.5 %copy.282 = bf16[2,4,4,24,4,768]{5,3,4,2,1,0:T(8,128)(2,1)} copy(bf16[2,4,4,24,4,768]{5,4,3,2,1,0:T(4,128)(2,1)} %reshape.337) | data formatting | bytes 9437184 | tf_op jit(solution)/shard_map/reshape | solution.py:469
  244.3 5.6 %fusion.6 = bf16[2,4,4,10,24,768]{5,4,3,2,1,0:T(8,128)(2,1)S(1)} fusion(bf16[2,4,4,1,1,768]{5,4,3,2,1,0:T(2,128)(2,1)S(1)} %reshape.354, bf16[2,4,4,4,24,768]{5,4,3,2,1,0:T(8,128)(2,1)} %bitcast.256, bf16[2,4,4,4,24,768]{5,4,3,2,1,0:T(8,128)(2,1)} %bitcast.240, bf16[2,4,4,1,24,768]{5,4,3,2,1,0:T(8,128)(2,1)} %bitcast.269), kind=kLoop, calls=%fused_computation.11 | loop fusion | flops 58982400 | bytes 22462464 | tf_op jit(solution)/shard_map/concatenate | solution.py:477
  263.1 41.7 %attend_back.1 = bf16[2048,1152]{1,0:T(8,128)(2,1)} custom-call(s32[8]{0:T(128)} %and_select_fusion.1.lo, s32[8]{0:T(128)} %and_select_fusion.hi, bf16[384,2048]{1,0:T(8,128)(2,1)} %fusion.21.query_t, bf16[2048,384]{1,0:T(8,128)(2,1)} %convolution_convert_fusion.3.keys, bf16[2048,384]{1,0:T(8,128)(2,1)} %add_convert_fusion.values, ...), custom_call_target="tpu_custom_call" | custom-call | flops 16106127360 | bytes 15728640 | tf_op jit(solution)/shard_map/attend_back/pallas_call | solution.py:236
  308.3 7.7 %convolution_convert_fusion.2 = bf16[768,1152]{1,0:T(8,128)(2,1)S(1)} fusion(bf16[2048,768]{1,0:T(8,128)(2,1)} %bitcast.259, bf16[2048,1152]{1,0:T(8,128)(2,1)} %attend_back.1), kind=kOutput, calls=%fused_computation.25 | convolution fusion | flops 3624763392 | bytes 9633792 | tf_op jit(solution)/shard_map/dot_general | solution.py:18
  318.9 11.9 %collective-permute-start.12 = (bf16[4,56,1152]{2,1,0:T(8,128)(2,1)}, bf16[4,56,1152]{2,1,0:T(8,128)(2,1)}, u32[]{:S(2)}, u32[]{:S(2)}) collective-permute-start(bf16[4,56,1152]{2,1,0:T(8,128)(2,1)} %get-tuple-element.148), channel_id=1, source_target_pairs={{0,2},{1,3},{2,0},{3,1},{4,6},{5,7},{6,4},{7,5},{8,10},{9,11},{10,... | collective-permute-start | bytes 1548296 | tf_op jit(solution)/shard_map/ppermute | solution.py:274
  331.9 4.4 fusion.23
  341.0 12.5 %collective-permute-done.12 = bf16[4,56,1152]{2,1,0:T(8,128)(2,1)} collective-permute-done((bf16[4,56,1152]{2,1,0:T(8,128)(2,1)}, bf16[4,56,1152]{2,1,0:T(8,128)(2,1)}, u32[]{:S(2)}, u32[]{:S(2)}) %collective-permute-start.12) | collective-permute-done | bytes 516128 | tf_op jit(solution)/shard_map/ppermute | solution.py:274
  358.1 5.8 %fusion.7 = bf16[4,4,10,24,768]{4,3,2,1,0:T(8,128)(2,1)S(1)} fusion(bf16[4,4,10,24,768]{4,3,2,1,0:T(8,128)(2,1)} %collective-permute-done.18, bf16[2,4,4,10,24,768]{5,4,3,2,1,0:T(8,128)(2,1)} %copy-done, s32[]{:T(128)S(6)} %select_n.152), kind=kLoop, calls=%fused_computation.13 | loop fusion | flops 11796480 | bytes 17694724 | tf_op jit(solution)/shard_map/convert_element_type | solution.py:479
  379.6 4.1 collective-permute-done.15
  404.0 29.7 %collective-permute-done.20 = bf16[4,10,24,768]{3,2,1,0:T(8,128)(2,1)} collective-permute-done((bf16[4,10,24,768]{3,2,1,0:T(8,128)(2,1)}, bf16[4,10,24,768]{3,2,1,0:T(8,128)(2,1)}, u32[]{:S(2)}, u32[]{:S(2)}) %collective-permute-start.20) | collective-permute-done | bytes 1474592 | tf_op jit(solution)/shard_map/ppermute | solution.py:274
  433.7 5.2 %fusion.59 = (bf16[4,10,24,768]{3,2,1,0:T(8,128)(2,1)S(1)}, f32[4,10,24,768]{3,2,1,0:T(8,128)}) fusion(bf16[4,10,24,768]{3,2,1,0:T(8,128)(2,1)} %collective-permute-done.21, bf16[4,10,24,768]{3,2,1,0:T(8,128)(2,1)} %collective-permute-done.20, bf16[4,10,24,768]{3,2,1,0:T(8,128)(2,1)} %collective-permute-done.19, bf16[4,4,10,24,768]{4,3,2,1,0:T(8,128)(2,1)} %copy-done.1, ...), kind=kLoop, calls=%fused_computation.194 | loop fusion | flops 5898240 | bytes 10321924 | tf_op jit(solution)/shard_map/convert_element_type | solution.py:320
  439.9 4.2 collective-permute-start.22
  445.6 4.6 fusion.17
  453.7 15.2 %collective-permute-done.22 = bf16[10,24,768]{2,1,0:T(8,128)(2,1)} collective-permute-done((bf16[10,24,768]{2,1,0:T(8,128)(2,1)}, bf16[10,24,768]{2,1,0:T(8,128)(2,1)}, u32[]{:S(2)}, u32[]{:S(2)}) %collective-permute-start.22) | collective-permute-done | bytes 368672 | tf_op jit(solution)/shard_map/ppermute | solution.py:281
  469.0 5.8 %collective-permute-done.23 = bf16[10,24,768]{2,1,0:T(8,128)(2,1)} collective-permute-done((bf16[10,24,768]{2,1,0:T(8,128)(2,1)}, bf16[10,24,768]{2,1,0:T(8,128)(2,1)}, u32[]{:S(2)}, u32[]{:S(2)}) %collective-permute-start.23) | collective-permute-done | bytes 368672 | tf_op jit(solution)/shard_map/ppermute | solution.py:281
  (285 shorter events, 142.4 us)
Async XLA Ops:
  7.2 125.2 %all-gather.3.cloned.1.call-start = ((), (), s32[]{:S(2)}) async-start(), calls=%async_computation | async-start | bytes 11354112 | tf_op jit(solution)/shard_map/all_gather | solution.py:393
  15.9 5.1 %collective-permute-start = (bf16[3,24,384]{2,1,0:T(8,128)(2,1)S(1)}, bf16[3,24,384]{2,1,0:T(8,128)(2,1)S(1)}, u32[]{:S(2)}, u32[]{:S(2)}) collective-permute-start(bf16[3,24,384]{2,1,0:T(8,128)(2,1)S(1)} %bitcast.299), channel_id=1, source_target_pairs={{0,16},{16,0},{1,17},{17,1},{2,18},{18,2},{3,19},{19,3},{4,20},{20... | collective-permute-start | bytes 165896 | tf_op jit(solution)/shard_map/ppermute | solution.py:269
  16.8 61.3 %collective-permute-start.7 = (bf16[1024,768]{0,1:T(8,128)(2,1)S(1)}, bf16[1024,768]{0,1:T(8,128)(2,1)}, u32[]{:S(2)}, u32[]{:S(2)}) collective-permute-start(bf16[1024,768]{0,1:T(8,128)(2,1)S(1)} %bitcast.264), channel_id=1, source_target_pairs={{0,16},{16,0},{1,17},{17,1},{2,18},{18,2},{3,19},{19,3},{4,20},{20... | collective-permute-start | bytes 4718600 | tf_op jit(solution)/shard_map/ppermute | solution.py:269
  21.1 7.3 %collective-permute-start.1 = (bf16[152,384]{1,0:T(8,128)(2,1)S(1)}, bf16[152,384]{1,0:T(8,128)(2,1)S(1)}, u32[]{:S(2)}, u32[]{:S(2)}) collective-permute-start(bf16[152,384]{1,0:T(8,128)(2,1)S(1)} %fusion.46), channel_id=1, source_target_pairs={{0,4},{1,5},{2,6},{3,7},{4,8},{5,9},{6,10},{7,11},{8,12},{9,13},{1... | collective-permute-start | bytes 350216 | tf_op jit(solution)/shard_map/ppermute | solution.py:281
  25.2 14.1 %collective-permute-start.2 = (bf16[152,384]{1,0:T(8,128)(2,1)S(1)}, bf16[152,384]{1,0:T(8,128)(2,1)S(1)}, u32[]{:S(2)}, u32[]{:S(2)}) collective-permute-start(bf16[152,384]{1,0:T(8,128)(2,1)S(1)} %fusion.46), channel_id=1, source_target_pairs={{0,8},{1,9},{2,10},{3,11},{4,12},{5,13},{6,14},{7,15},{8,0},{9,1},... | collective-permute-start | bytes 350216 | tf_op jit(solution)/shard_map/ppermute | solution.py:281
  26.5 14.9 %collective-permute-start.3 = (bf16[152,384]{1,0:T(8,128)(2,1)S(1)}, bf16[152,384]{1,0:T(8,128)(2,1)S(1)}, u32[]{:S(2)}, u32[]{:S(2)}) collective-permute-start(bf16[152,384]{1,0:T(8,128)(2,1)S(1)} %fusion.46), channel_id=1, source_target_pairs={{0,12},{1,13},{2,14},{3,15},{4,0},{5,1},{6,2},{7,3},{8,4},{9,5},{1... | collective-permute-start | bytes 350216 | tf_op jit(solution)/shard_map/ppermute | solution.py:281
  41.4 18.2 %collective-permute-start.4 = (bf16[4,152,384]{2,1,0:T(8,128)(2,1)S(1)}, bf16[4,152,384]{2,1,0:T(8,128)(2,1)S(1)}, u32[]{:S(2)}, u32[]{:S(2)}) collective-permute-start(bf16[4,152,384]{2,1,0:T(8,128)(2,1)S(1)} %bitcast_dynamic-update-slice_fusion.7), channel_id=1, source_target_pairs={{0,1},{1,0},{2,3},{3,2},{4,5},{5,4},{6,7},{7,6},{8,9},{9,8},{10,11... | collective-permute-start | bytes 1400840 | tf_op jit(solution)/shard_map/ppermute | solution.py:274
  42.2 18.7 %collective-permute-start.5 = (bf16[4,152,384]{2,1,0:T(8,128)(2,1)S(1)}, bf16[4,152,384]{2,1,0:T(8,128)(2,1)S(1)}, u32[]{:S(2)}, u32[]{:S(2)}) collective-permute-start(bf16[4,152,384]{2,1,0:T(8,128)(2,1)S(1)} %bitcast_dynamic-update-slice_fusion.7), channel_id=1, source_target_pairs={{0,2},{1,3},{2,0},{3,1},{4,6},{5,7},{6,4},{7,5},{8,10},{9,11},{10,... | collective-permute-start | bytes 1400840 | tf_op jit(solution)/shard_map/ppermute | solution.py:274
  44.1 30.5 %collective-permute-start.6 = (bf16[4,152,384]{2,1,0:T(8,128)(2,1)S(1)}, bf16[4,152,384]{2,1,0:T(8,128)(2,1)S(1)}, u32[]{:S(2)}, u32[]{:S(2)}) collective-permute-start(bf16[4,152,384]{2,1,0:T(8,128)(2,1)S(1)} %bitcast_dynamic-update-slice_fusion.7), channel_id=1, source_target_pairs={{0,3},{1,2},{2,1},{3,0},{4,7},{5,6},{6,5},{7,4},{8,11},{9,10},{10,... | collective-permute-start | bytes 1400840 | tf_op jit(solution)/shard_map/ppermute | solution.py:274
  128.3 2.8 collective-permute-start.8
  243.7 16.9 %collective-permute-start.9 = (bf16[1024,384]{1,0:T(8,128)(2,1)S(1)}, bf16[1024,384]{1,0:T(8,128)(2,1)}, u32[]{:S(2)}, u32[]{:S(2)}) collective-permute-start(bf16[1024,384]{1,0:T(8,128)(2,1)S(1)} %bitcast.275), channel_id=1, source_target_pairs={{0,16},{16,0},{1,17},{17,1},{2,18},{18,2},{3,19},{19,3},{4,20},{20... | collective-permute-start | bytes 2359304 | tf_op jit(solution)/shard_map/ppermute | solution.py:269
  256.9 101.1 %collective-permute-start.18 = (bf16[4,4,10,24,768]{4,3,2,1,0:T(8,128)(2,1)}, bf16[4,4,10,24,768]{4,3,2,1,0:T(8,128)(2,1)}, u32[]{:S(2)}, u32[]{:S(2)}) collective-permute-start(bf16[4,4,10,24,768]{4,3,2,1,0:T(8,128)(2,1)} %dynamic-slice_bitcast_fusion), channel_id=1, source_target_pairs={{0,16},{16,0},{1,17},{17,1},{2,18},{18,2},{3,19},{19,3},{4,20},{20... | collective-permute-start | bytes 17694728 | tf_op jit(solution)/shard_map/ppermute | solution.py:269
  304.8 27.1 %slice-start = ((s8[4718592]{0:T(1024)(128)(4,1)}), s8[524288]{0:T(1024)(128)(4,1)S(1)}, s32[]{:S(2)}) async-start(s8[4718592]{0:T(1024)(128)(4,1)} %bitcast.248), calls=%async_computation.1 | async-start | bytes 1048576
  308.3 23.5 %slice-start.1 = ((s8[4718592]{0:T(1024)(128)(4,1)}), s8[4194304]{0:T(1024)(128)(4,1)S(1)}, s32[]{:S(2)}) async-start(s8[4718592]{0:T(1024)(128)(4,1)} %bitcast.248), calls=%async_computation.2 | async-start | bytes 8388608
  316.2 15.7 %copy-start.23 = (bf16[1,2,4,4,24,384]{5,4,3,2,1,0:T(8,128)(2,1)S(1)}, bf16[1,2,4,4,24,384]{5,4,3,2,1,0:T(8,128)(2,1)}, u32[]{:S(2)}) copy-start(bf16[1,2,4,4,24,384]{5,4,3,2,1,0:T(8,128)(2,1)} %copy.222) | copy-start | bytes 1769476
  316.2 15.6 %copy-start.25 = (bf16[1,2,4,4,24,384]{5,4,3,2,1,0:T(8,128)(2,1)S(1)}, bf16[1,2,4,4,24,384]{5,4,3,2,1,0:T(8,128)(2,1)}, u32[]{:S(2)}) copy-start(bf16[1,2,4,4,24,384]{5,4,3,2,1,0:T(8,128)(2,1)} %copy.218) | copy-start | bytes 1769476
  316.2 15.6 %copy-start.27 = (bf16[1,2,4,4,24,384]{5,4,3,2,1,0:T(8,128)(2,1)S(1)}, bf16[1,2,4,4,24,384]{5,4,3,2,1,0:T(8,128)(2,1)}, u32[]{:S(2)}) copy-start(bf16[1,2,4,4,24,384]{5,4,3,2,1,0:T(8,128)(2,1)} %copy.221) | copy-start | bytes 1769476
  318.9 22.1 %collective-permute-start.11 = (bf16[4,56,1152]{2,1,0:T(8,128)(2,1)}, bf16[4,56,1152]{2,1,0:T(8,128)(2,1)}, u32[]{:S(2)}, u32[]{:S(2)}) collective-permute-start(bf16[4,56,1152]{2,1,0:T(8,128)(2,1)} %get-tuple-element.146), channel_id=1, source_target_pairs={{0,1},{1,0},{2,3},{3,2},{4,5},{5,4},{6,7},{7,6},{8,9},{9,8},{10,11... | collective-permute-start | bytes 1548296 | tf_op jit(solution)/shard_map/ppermute | solution.py:274
  318.9 34.6 %collective-permute-start.12 = (bf16[4,56,1152]{2,1,0:T(8,128)(2,1)}, bf16[4,56,1152]{2,1,0:T(8,128)(2,1)}, u32[]{:S(2)}, u32[]{:S(2)}) collective-permute-start(bf16[4,56,1152]{2,1,0:T(8,128)(2,1)} %get-tuple-element.148), channel_id=1, source_target_pairs={{0,2},{1,3},{2,0},{3,1},{4,6},{5,7},{6,4},{7,5},{8,10},{9,11},{10,... | collective-permute-start | bytes 1548296 | tf_op jit(solution)/shard_map/ppermute | solution.py:274
  330.8 24.5 %collective-permute-start.13 = (bf16[4,56,1152]{2,1,0:T(8,128)(2,1)}, bf16[4,56,1152]{2,1,0:T(8,128)(2,1)}, u32[]{:S(2)}, u32[]{:S(2)}) collective-permute-start(bf16[4,56,1152]{2,1,0:T(8,128)(2,1)} %get-tuple-element.147), channel_id=1, source_target_pairs={{0,3},{1,2},{2,1},{3,0},{4,7},{5,6},{6,5},{7,4},{8,11},{9,10},{10,... | collective-permute-start | bytes 1548296 | tf_op jit(solution)/shard_map/ppermute | solution.py:274
  340.9 104.7 %collective-permute-start.10 = (f32[1024,768]{0,1:T(8,128)}, f32[1024,768]{0,1:T(8,128)}, u32[]{:S(2)}, u32[]{:S(2)}) collective-permute-start(f32[1024,768]{0,1:T(8,128)} %bitcast.257), channel_id=1, source_target_pairs={{0,16},{16,0},{1,17},{17,1},{2,18},{18,2},{3,19},{19,3},{4,20},{20... | collective-permute-start | bytes 9437192 | tf_op jit(solution)/shard_map/ppermute | solution.py:269
  363.9 22.6 %copy-start.10 = (bf16[1,1024,768]{1,2,0:T(8,128)(2,1)S(1)}, bf16[1,1024,768]{1,2,0:T(8,128)(2,1)}, u32[]{:S(2)}) copy-start(bf16[1,1024,768]{1,2,0:T(8,128)(2,1)} %get-tuple-element.145) | copy-start | bytes 4718596
  367.7 36.2 %collective-permute-start.19 = (bf16[4,10,24,768]{3,2,1,0:T(8,128)(2,1)}, bf16[4,10,24,768]{3,2,1,0:T(8,128)(2,1)}, u32[]{:S(2)}, u32[]{:S(2)}) collective-permute-start(bf16[4,10,24,768]{3,2,1,0:T(8,128)(2,1)} %get-tuple-element.142), channel_id=1, source_target_pairs={{0,1},{1,0},{2,3},{3,2},{4,5},{5,4},{6,7},{7,6},{8,9},{9,8},{10,11... | collective-permute-start | bytes 4423688 | tf_op jit(solution)/shard_map/ppermute | solution.py:274
  368.3 65.4 %collective-permute-start.20 = (bf16[4,10,24,768]{3,2,1,0:T(8,128)(2,1)}, bf16[4,10,24,768]{3,2,1,0:T(8,128)(2,1)}, u32[]{:S(2)}, u32[]{:S(2)}) collective-permute-start(bf16[4,10,24,768]{3,2,1,0:T(8,128)(2,1)} %get-tuple-element.144), channel_id=1, source_target_pairs={{0,2},{1,3},{2,0},{3,1},{4,6},{5,7},{6,4},{7,5},{8,10},{9,11},{10,... | collective-permute-start | bytes 4423688 | tf_op jit(solution)/shard_map/ppermute | solution.py:274
  370.1 63.6 %collective-permute-start.21 = (bf16[4,10,24,768]{3,2,1,0:T(8,128)(2,1)}, bf16[4,10,24,768]{3,2,1,0:T(8,128)(2,1)}, u32[]{:S(2)}, u32[]{:S(2)}) collective-permute-start(bf16[4,10,24,768]{3,2,1,0:T(8,128)(2,1)} %get-tuple-element.143), channel_id=1, source_target_pairs={{0,3},{1,2},{2,1},{3,0},{4,7},{5,6},{6,5},{7,4},{8,11},{9,10},{10,... | collective-permute-start | bytes 4423688 | tf_op jit(solution)/shard_map/ppermute | solution.py:274
  371.9 5.7 %collective-permute-start.14 = (bf16[56,1152]{1,0:T(8,128)(2,1)S(1)}, bf16[56,1152]{1,0:T(8,128)(2,1)S(1)}, u32[]{:S(2)}, u32[]{:S(2)}) collective-permute-start(bf16[56,1152]{1,0:T(8,128)(2,1)S(1)} %get-tuple-element.167), channel_id=1, source_target_pairs={{0,4},{1,5},{2,6},{3,7},{4,8},{5,9},{6,10},{7,11},{8,12},{9,13},{1... | collective-permute-start | bytes 387080 | tf_op jit(solution)/shard_map/ppermute | solution.py:281
  377.7 5.9 %collective-permute-start.15 = (bf16[56,1152]{1,0:T(8,128)(2,1)S(1)}, bf16[56,1152]{1,0:T(8,128)(2,1)S(1)}, u32[]{:S(2)}, u32[]{:S(2)}) collective-permute-start(bf16[56,1152]{1,0:T(8,128)(2,1)S(1)} %get-tuple-element.169), channel_id=1, source_target_pairs={{0,8},{1,9},{2,10},{3,11},{4,12},{5,13},{6,14},{7,15},{8,0},{9,1},... | collective-permute-start | bytes 387080 | tf_op jit(solution)/shard_map/ppermute | solution.py:281
  383.6 6.8 %collective-permute-start.16 = (bf16[56,1152]{1,0:T(8,128)(2,1)}, bf16[56,1152]{1,0:T(8,128)(2,1)S(1)}, u32[]{:S(2)}, u32[]{:S(2)}) collective-permute-start(bf16[56,1152]{1,0:T(8,128)(2,1)} %get-tuple-element.168), channel_id=1, source_target_pairs={{0,12},{1,13},{2,14},{3,15},{4,0},{5,1},{6,2},{7,3},{8,4},{9,5},{1... | collective-permute-start | bytes 387080 | tf_op jit(solution)/shard_map/ppermute | solution.py:281
  394.6 3.9 collective-permute-start.17
  439.9 29.1 %collective-permute-start.22 = (bf16[10,24,768]{2,1,0:T(8,128)(2,1)}, bf16[10,24,768]{2,1,0:T(8,128)(2,1)}, u32[]{:S(2)}, u32[]{:S(2)}) collective-permute-start(bf16[10,24,768]{2,1,0:T(8,128)(2,1)} %get-tuple-element.156), channel_id=1, source_target_pairs={{0,4},{1,5},{2,6},{3,7},{4,8},{5,9},{6,10},{7,11},{8,12},{9,13},{1... | collective-permute-start | bytes 1105928 | tf_op jit(solution)/shard_map/ppermute | solution.py:281
  444.1 30.6 %collective-permute-start.23 = (bf16[10,24,768]{2,1,0:T(8,128)(2,1)}, bf16[10,24,768]{2,1,0:T(8,128)(2,1)}, u32[]{:S(2)}, u32[]{:S(2)}) collective-permute-start(bf16[10,24,768]{2,1,0:T(8,128)(2,1)} %get-tuple-element.158), channel_id=1, source_target_pairs={{0,8},{1,9},{2,10},{3,11},{4,12},{5,13},{6,14},{7,15},{8,0},{9,1},... | collective-permute-start | bytes 1105928 | tf_op jit(solution)/shard_map/ppermute | solution.py:281
  444.1 30.6 %collective-permute-start.24 = (bf16[10,24,768]{2,1,0:T(8,128)(2,1)S(1)}, bf16[10,24,768]{2,1,0:T(8,128)(2,1)}, u32[]{:S(2)}, u32[]{:S(2)}) collective-permute-start(bf16[10,24,768]{2,1,0:T(8,128)(2,1)S(1)} %get-tuple-element.157), channel_id=1, source_target_pairs={{0,12},{1,13},{2,14},{3,15},{4,0},{5,1},{6,2},{7,3},{8,4},{9,5},{1... | collective-permute-start | bytes 1105928 | tf_op jit(solution)/shard_map/ppermute | solution.py:281
  (30 other events, 173.1 us)
Sparse Core Ops, SparseCore 0:
  14.9 105.7 all-gather.2
